TPU v7x, 256 devices: a whole 4x4x8 slice. The times are simulated.
256 devices in a mesh: gx: 16 (over z_lo, x), gy: 8 (over y, z_hi), gz: 2 (over core).
Axes of the slice: x: 4, y: 4, z: 8 (z_hi: 2, z_lo: 4; z = z_hi * 4 + z_lo), core: 2. Of those that a mesh axis runs over, the one named last changes fastest.
Arguments:
- pressure: float32 [128, 256, 256], P('gx', 'gy', 'gz'), may hold values from -6 to 6
- accumulation: float32 [128, 256, 256], P('gx', 'gy', 'gz'), may hold values from 0.05 to 0.5
- trans_x: float32 [128, 256, 256], P('gx', 'gy', 'gz'), may hold values from 0.1 to 1
- trans_y: float32 [128, 256, 256], P('gx', 'gy', 'gz'), may hold values from 0.1 to 1
- trans_z: float32 [128, 256, 256], P('gx', 'gy', 'gz'), may hold values from 0.1 to 1
- source: float32 [128, 256, 256], P('gx', 'gy', 'gz'), may hold values from -6 to 6
- well_cells: int32 [1024], replicated, may hold values from 0 to 8388607
- well_rates: float32 [1024], replicated, may hold values from -16 to 16
- basis: bfloat16 [6, 12, 12, 16, 32, 64], P(None, None, None, 'gx', 'gy', 'gz'), may hold values from 0 to 0.099609375
- coarse_off: float32 [26, 16, 32, 64], P(None, 'gx', 'gy', 'gz'), may hold values from -0.1 to -0.02
- coarse_diag: float32 [16, 32, 64], P('gx', 'gy', 'gz'), may hold values from 3 to 6
Outputs:
- residual: float32 [128, 256, 256], P('gx', 'gy', 'gz')
- coarse_solution: float32 [16, 32, 64], P('gx', 'gy', 'gz')
- new_pressure: float32 [128, 256, 256], P('gx', 'gy', 'gz')
All inputs are finite; a program needn't handle non-finite values.
Results may differ from a plain program's by a relative error of at most 0.0004.
Values may be sent and summed in bfloat16 or wider, within the bound.
No kernel may reach another device: no remote copies, remote signals or barrier semaphores. Data moves between devices by JAX's collectives and lax.ppermute only.
A program may use at most 128 MiB of HBM per device.

v0:
```python
import jax
import jax.numpy as jnp
from jax import lax
from jax.experimental import pallas as pl
from jax.experimental.pallas import tpu as pltpu
from jax.sharding import PartitionSpec as P


damping = 0.8
F32 = jnp.float32
BF16 = jnp.bfloat16


def iota(shape, dim):
    return lax.broadcasted_iota(jnp.int32, shape, dim)


def parts(a):
    high = a.astype(BF16)
    rest = a - high.astype(F32)
    middle = rest.astype(BF16)
    low = (rest - middle.astype(F32)).astype(BF16)
    return high, middle, low


NN = (((1,), (0,)), ((), ()))
NT = (((1,), (1,)), ((), ()))


def dot(a, b, dims=NN):
    return lax.dot_general(a, b, dims, preferred_element_type=F32)


def dot3(a, b, dims=NN):
    high, middle, low = parts(a)
    return dot(high, b, dims) + dot(middle, b, dims) + dot(low, b, dims)


def spread(core):
    lane = iota((128, 128), 0)
    block = iota((128, 128), 1)
    block = jnp.where(block < 64, block, 32 - core)
    own = core * 32 + lane // 4
    inside = jnp.where(block == own, 1.0, 0.0).astype(BF16)
    below = (lane % 4 == 0) & (block == own - 1)
    above = (lane % 4 == 3) & (block == own + 1)
    return inside, jnp.where(below | above, 1.0, 0.0).astype(BF16)


def faced(core, mine, theirs):
    lane = iota(mine.shape, 1)
    return mine + jnp.where(lane == 127 - 127 * core, pltpu.roll(theirs, 126 + core, 1), 0.0)


def pack_kernel(
    basis_in, pressure_in, trans_y_in, coarse_off_in, coarse_diag_in, wo, wz, to_next_y, to_prev_y, coarse,
    basis, pressure, trans_y, coarse_off, coarse_diag, done,
):
    copies = [
        pltpu.make_async_copy(source, target, done.at[n])
        for n, (source, target) in enumerate(
            (
                (basis_in, basis),
                (coarse_off_in, coarse_off),
                (coarse_diag_in, coarse_diag),
                (pressure_in, pressure),
                (trans_y_in, trans_y),
            )
        )
    ]
    for copy in copies:
        copy.start()
    core = lax.axis_index("gz")
    block = iota((32, 128), 0)
    lane = iota((32, 128), 1)

    def place(mask):
        return jnp.where(mask, 1.0, 0.0).astype(BF16)

    for copy in copies:
        copy.wait()
    total = dot(basis[1], place(lane == 4 * block))
    for k in (2, 3, 4):
        total = total + dot(basis[k], place(lane == 4 * block + (k - 1)))
    wo[...] = total
    wz[...] = dot(basis[5], place((lane == 4 * block + 4) | ((block == 31) & (lane == 1) & (core == 0)))) + dot(
        basis[0], place((lane == 4 * block - 1) | ((block == 0) & (lane == 1) & (core == 1)))
    )
    for n in range(2):
        for half, w in enumerate((wo, wz)):
            spot = (2 * n + half) * 12
            to_next_y[pl.ds(spot, 12), :] = w[pl.ds((10 + n) * 48 + 3, 12, stride=4), :]
            to_prev_y[pl.ds(spot, 12), :] = w[pl.ds(n * 48, 12, stride=4), :]
    for x in range(8):
        to_next_y[pl.ds(48 + x, 1), :] = pressure[x, pl.ds(31, 1), :]
        to_next_y[pl.ds(56 + x, 1), :] = trans_y[x, pl.ds(31, 1), :]
        to_prev_y[pl.ds(48 + x, 1), :] = pressure[x, pl.ds(0, 1), :]
    inverse = damping / coarse_diag[0]
    total = jnp.zeros((26, 128), F32)
    line = jnp.zeros((1, 128), F32)
    for by in range(4):
        spot = place(lane == 32 * by + block)
        scale = inverse[by : by + 1]
        total = total + dot3(coarse_off[:, 0, by, :] * scale, spot)
        line = line + dot3(jnp.broadcast_to(scale, (8, 32)), spot)[0:1]
    coarse[...] = jnp.zeros_like(coarse)
    coarse[pl.ds(0, 26), :] = total
    coarse[pl.ds(26, 1), :] = line
    to_next_y[pl.ds(64, 32), :] = coarse[...]
    to_prev_y[pl.ds(56, 32), :] = coarse[...]


def relay_kernel(wo, wz, facing, pressure, trans_x, coarse, from_prev_y, from_next_y, whole, to_next_x, to_prev_x, strips):
    core = lax.axis_index("gz")
    whole[...] = faced(core, wz[...], facing[...])
    for j in range(12):
        for half, w in enumerate((wo, whole)):
            to_next_x[pl.ds(96 * half + 8 * j, 8), :] = w[pl.ds(48 * j + 40, 8), :]
            to_prev_x[pl.ds(96 * half + 8 * j, 8), :] = w[pl.ds(48 * j, 8), :]
    to_next_x[pl.ds(192, 32), :] = pressure[7]
    to_prev_x[pl.ds(192, 32), :] = pressure[0]
    for side, strip in enumerate((from_prev_y, from_next_y)):
        for n in range(2):
            strips[pl.ds(side * 24 + n * 12, 12), :] = strip[pl.ds((2 * n + 1) * 12, 12), :]
        for spot in range(4):
            to_next_x[pl.ds(224 + side * 8 + spot * 2, 2), :] = strip[pl.ds(spot * 12 + 10, 2), :]
            to_prev_x[pl.ds(224 + side * 8 + spot * 2, 2), :] = strip[pl.ds(spot * 12, 2), :]
    for ref in (to_next_x, to_prev_x):
        ref[pl.ds(240, 32), :] = from_prev_y[pl.ds(64, 32), :]
        ref[pl.ds(272, 32), :] = coarse[...]
        ref[pl.ds(304, 32), :] = from_next_y[pl.ds(56, 32), :]
    to_next_x[pl.ds(336, 32), :] = trans_x[7]


def collect_kernel(from_prev_x, from_next_x, own, corners, up, down):
    corners[pl.ds(0, 16), :] = from_prev_x[pl.ds(224, 16), :]
    corners[pl.ds(16, 16), :] = from_next_x[pl.ds(224, 16), :]
    at = iota((96, 128), 0) % 32

    def narrow(rows):
        rest = rows - rows.astype(BF16).astype(F32)
        return jnp.where(at == 27, pltpu.roll(rest, 1, 0), rows).astype(BF16)

    for ref, far, near in ((up, from_prev_x, from_next_x), (down, from_next_x, from_prev_x)):
        outer = narrow(far[pl.ds(240, 96), :]).astype(F32)
        inverses = [outer[32 * yc + 24 : 32 * yc + 32] for yc in range(3)]
        ref[pl.ds(0, 32), :] = jnp.concatenate(inverses + [jnp.zeros((8, 128), F32)], axis=0).astype(BF16)
        ref[pl.ds(32, 96), :] = narrow(own[pl.ds(240, 96), :])
        ref[pl.ds(128, 96), :] = narrow(near[pl.ds(240, 96), :])


def window_kernel(up, down, from_prev_x, own, from_next_x, near):
    def wide(rows):
        rows = rows.astype(F32)
        at = iota(rows.shape, 0) % 32
        return rows + jnp.where(at == 26, pltpu.roll(rows, rows.shape[0] - 1, 0), 0.0)

    for spot, ref in ((0, up), (680, down)):
        near[pl.ds(spot, 8), :] = jnp.zeros((8, 128), F32)
        outer = ref[pl.ds(0, 32), :].astype(F32)
        for yc in range(3):
            near[pl.ds(spot + yc, 1), :] = outer[8 * yc + 2 : 8 * yc + 3] + outer[8 * yc + 3 : 8 * yc + 4]
    near[pl.ds(8, 96), :] = wide(up[pl.ds(32, 96), :])
    near[pl.ds(104, 96), :] = wide(up[pl.ds(128, 96), :])
    near[pl.ds(200, 96), :] = from_prev_x[pl.ds(240, 96), :]
    near[pl.ds(296, 96), :] = own[pl.ds(240, 96), :]
    near[pl.ds(392, 96), :] = from_next_x[pl.ds(240, 96), :]
    near[pl.ds(488, 96), :] = wide(down[pl.ds(128, 96), :])
    near[pl.ds(584, 96), :] = wide(down[pl.ds(32, 96), :])


def stack_kernel(near, far, coefs):
    core = lax.axis_index("gz")
    coefs[pl.ds(pl.multiple_of(core * 688, 8), 688), :] = near[...]
    coefs[pl.ds(pl.multiple_of((1 - core) * 688, 8), 688), :] = far[...]


def wells_kernel(cells, rates, wells):
    gx = lax.axis_index("gx")
    gy = lax.axis_index("gy")
    core = lax.axis_index("gz")
    rows_at = iota((256, 128), 0)
    lane_at = iota((128, 128), 0)
    total = jnp.zeros((256, 128), F32)
    for c in range(8):
        cell = cells[pl.ds(c, 1), :]
        at_x = (cell >> 16) - gx * 8
        at_y = ((cell >> 8) & 255) - gy * 32
        at_z = (cell & 255) - core * 128
        inside = (at_x >= 0) & (at_x < 8) & (at_y >= 0) & (at_y < 32)
        row = jnp.where(inside, at_x * 32 + at_y, -1)
        hit = jnp.where(row == rows_at, 1.0, 0.0).astype(BF16)
        here = at_z == lane_at
        for part in parts(rates[pl.ds(c, 1), :]):
            total = total + dot(hit, jnp.where(here, part.astype(F32), 0.0).astype(BF16), NT)
    wells[...] = total


def local_kernel(
    pressure, accumulation, trans_x, trans_y, trans_z, source, wells, facing_p, facing_t, from_prev_y, from_next_y, partial
):
    gy = lax.axis_index("gy")
    core = lax.axis_index("gz")
    size_y = lax.axis_size("gy")
    row = iota((32, 128), 0)
    lane = iota((32, 128), 1)
    has_next_y = jnp.where(gy < size_y - 1, 1.0, 0.0)
    has_prev_y = jnp.where(gy > 0, 1.0, 0.0)
    has_next_z = jnp.where(core == 0, 1.0, 0.0)
    has_prev_z = jnp.where(core == 1, 1.0, 0.0)
    for x in range(8):
        here = pressure[x]
        flux = jnp.zeros((32, 128), F32)
        if x < 7:
            flux = flux + trans_x[x] * (here - pressure[x + 1])
        if x > 0:
            flux = flux + trans_x[x - 1] * (here - pressure[x - 1])
        after = jnp.where(row == 31, from_next_y[pl.ds(48 + x, 1), :] * has_next_y, pltpu.roll(here, 31, 0))
        before = jnp.where(row == 0, from_prev_y[pl.ds(48 + x, 1), :] * has_prev_y, pltpu.roll(here, 1, 0))
        t_here = trans_y[x]
        t_before = jnp.where(row == 0, from_prev_y[pl.ds(56 + x, 1), :] * has_prev_y, pltpu.roll(t_here, 1, 0))
        flux = flux + t_here * (here - after) + t_before * (here - before)
        other = facing_p[x]
        after = jnp.where(lane == 127, pltpu.roll(other, 127, 1) * has_next_z, pltpu.roll(here, 127, 1))
        before = jnp.where(lane == 0, pltpu.roll(other, 1, 1) * has_prev_z, pltpu.roll(here, 1, 1))
        t_here = trans_z[x]
        t_before = jnp.where(lane == 0, pltpu.roll(facing_t[x], 1, 1) * has_prev_z, pltpu.roll(t_here, 1, 1))
        flux = flux + t_here * (here - after) + t_before * (here - before)
        partial[x] = source[x] + wells[pl.ds(32 * x, 32), :] - accumulation[x] * here - flux


def sums_kernel(
    partial, pressure, trans_x, wo, wz, from_prev_x, from_next_x, from_prev_y, from_next_y, facing_y,
    residual, field, sums_o, sums_z,
):
    gx = lax.axis_index("gx")
    core = lax.axis_index("gz")
    size_x = lax.axis_size("gx")
    has_next_x = jnp.where(gx < size_x - 1, 1.0, 0.0)
    has_prev_x = jnp.where(gx > 0, 1.0, 0.0)
    field[...] = jnp.zeros_like(field)
    for x in range(8):
        value = partial[x]
        here = pressure[x]
        if x == 0:
            value = value - from_prev_x[pl.ds(336, 32), :] * has_prev_x * (
                here - from_prev_x[pl.ds(192, 32), :] * has_prev_x
            )
        if x == 7:
            value = value - trans_x[7] * (here - from_next_x[pl.ds(192, 32), :] * has_next_x)
        residual[x] = value
        field[pl.ds(40 * x + 2, 32), :] = value
    sums_o[...] = jnp.zeros_like(sums_o)
    sums_z[...] = jnp.zeros_like(sums_z)
    columns = (
        [(from_prev_x, 0, 96, 8, il * 4, il) for il in range(2)],
        [(None, 0, 0, 48, (x + 2) * 4, x) for x in range(8)],
        [(from_next_x, 0, 96, 8, il * 4, 6 + il) for il in range(2)],
    )
    for column, entries in enumerate(columns):
        for by in range(4):
            totals = [None, None]
            for ref, base_o, base_z, step, start, x in entries:
                upper = field[pl.ds(40 * x + 8 * by, 8), :]
                lower = field[pl.ds(40 * x + 8 * by + 8, 4), :]
                for half in range(2):
                    w = ref if ref is not None else (wo, wz)[half]
                    first = (base_o, base_z)[half] + start + by
                    w8 = w[pl.ds(first, 8, stride=step), :]
                    w4 = w[pl.ds(first + 8 * step, 4, stride=step), :]
                    terms = (w8 * upper, w4 * lower)
                    if totals[half] is None:
                        totals[half] = terms
                    else:
                        totals[half] = tuple(a + b for a, b in zip(totals[half], terms))
            for half, sums in enumerate((sums_o, sums_z)):
                a8, a4 = totals[half]
                line = jnp.sum(a8, axis=0, keepdims=True) + jnp.sum(a4, axis=0, keepdims=True)
                sums[pl.ds((by + 1) * 8 + column, 1), :] = line
    for side, (by, first_row, strip) in enumerate(((-1, 2, from_prev_y), (4, 32, from_next_y))):
        for half, sums in enumerate((sums_o, sums_z)):
            total = None
            for n in range(2):
                tile = strip[pl.ds((2 * n + half) * 12 + 2, 8), :]
                if half:
                    tile = faced(core, tile, facing_y[pl.ds(side * 24 + n * 12 + 2, 8), :])
                line = tile * field[pl.ds(first_row + n, 8, stride=40), :]
                total = line if total is None else total + line
            sums[pl.ds((by + 1) * 8 + 1, 1), :] = jnp.sum(total, axis=0, keepdims=True)


def tail_kernel(field, sums_o, sums_z, corners, facing_x, message, whole, done_o, done_z, pattern):
    core = lax.axis_index("gz")
    at = iota((32, 128), 0)
    whole[...] = jnp.where((at % 8) // 2 % 2 == 1, faced(core, corners[...], facing_x[...]), corners[...])
    done_o[...] = sums_o[...]
    done_z[...] = sums_z[...]
    for side, (by, first_row) in enumerate(((-1, 2), (4, 32))):
        for half, sums in enumerate((done_o, done_z)):
            for column, first_x in ((0, 0), (2, 6)):
                total = None
                for n in range(2):
                    tile = whole[pl.ds(column * 8 + side * 8 + (2 * n + half) * 2, 2), :]
                    line = tile * field[pl.ds(40 * first_x + first_row + n, 2, stride=40), :]
                    total = line if total is None else total + line
                sums[pl.ds((by + 1) * 8 + column, 1), :] = jnp.sum(total, axis=0, keepdims=True)
    inside, reach = spread(core)
    out = dot3(done_o[...], inside) + dot3(done_z[...], reach)
    level = [out[8 * n : 8 * n + 8] for n in range(6)]
    group = iota((8, 128), 1) // 32
    group1 = iota((1, 128), 1) // 32
    halves = []
    for zc in range(2):
        total = jnp.zeros((8, 128), F32)
        for by in range(4):
            shift = (by * 32 - zc * 32) % 128
            moved = pltpu.roll(level[by + 1], shift, 1) if shift else level[by + 1]
            total = jnp.where(group == by, moved, total)
        hooks = [[], []]
        for n in range(4):
            shift = (n * 32 - zc * 32) % 128
            value = level[5] if n % 2 == 0 else level[0]
            value = pltpu.roll(value, shift, 1) if shift else value
            hooks[0].append(value[n // 2 : n // 2 + 1])
            hooks[1].append(value[2:3])
        fourth = jnp.where(
            group1 == 0, hooks[0][0], jnp.where(group1 == 1, hooks[0][1], jnp.where(group1 == 2, hooks[0][2], hooks[0][3]))
        )
        fifth = jnp.where(group1 == 0, hooks[1][0], hooks[1][1])
        halves.append((total[0:3], fourth, fifth))
    first = core == 0
    row = iota((48, 128), 0)
    mask = (iota((48, 128), 1) == 64 + (row // 8) * 4 + row % 8) & (row % 8 < 3)
    across = jnp.sum(jnp.where(mask, out, 0.0), axis=0, keepdims=True)
    for n in range(8):
        pattern[pl.ds(5 * n, 3), :] = jnp.where(first, halves[0][0], halves[1][0])
        pattern[pl.ds(5 * n + 3, 1), :] = jnp.where(first, halves[0][1], halves[1][1])
        pattern[pl.ds(5 * n + 4, 1), :] = jnp.where(
            group1 < 2, jnp.where(first, halves[0][2], halves[1][2]), across
        )
    block = pattern[...]
    for n in range(message.shape[0] // 40):
        message[pl.ds(40 * n, 40), :] = block


def gather_kernel(shared, own, padded):
    gx = lax.axis_index("gx")
    gy = lax.axis_index("gy")
    core = lax.axis_index("gz")
    size_x = lax.axis_size("gx")
    padded[...] = jnp.zeros_like(padded)
    for x in range(size_x):
        padded[pl.ds((x + 5) * 60 + 10, 40), :] = shared[pl.ds(x * 40, 40), :]
    lane = iota((9, 128), 1)
    source = iota((128, 128), 0)
    target = iota((128, 128), 1)
    edge = 31 * core
    at = target // 32
    hit = target % 32 == edge

    def place(mask):
        return jnp.where(mask, 1.0, 0.0).astype(BF16)

    within = place(hit & (source == 68 + 4 * at))
    lower = place(hit & (at == 0) & (source == 84))
    upper = place(hit & (at == 3) & (source == 64))

    def line(dx, dy, kind):
        return padded[pl.ds(((gx + 1 + dx) * 12 + gy + 2 + dy) * 5 + kind, 9, stride=60), :]

    beyond, before, across = [], [], []
    for dy in range(-2, 3):
        a, b, c, d, e = line(1, dy, 3), line(0, dy, 3), line(-1, dy, 4), line(1, dy, 4), line(0, dy, 4)
        beyond.append(a + pltpu.roll(b, 64, 1) + c)
        before.append(pltpu.roll(a, 64, 1) + b + pltpu.roll(c, 64, 1))
        across.append(d + pltpu.roll(e, 127, 1) + pltpu.roll(c, 126, 1))
    own[...] = jnp.zeros_like(own)
    for yc in range(3):
        total = line(1, yc - 1, 0) + line(0, yc - 1, 1) + line(-1, yc - 1, 2)
        total = total + jnp.where(lane < 32, beyond[yc], jnp.where(lane >= 96, before[yc + 2], 0.0))
        own[pl.ds(16 * yc, 9), :] = total
        own[pl.ds(48 + 16 * yc, 9), :] = (
            dot3(across[yc + 1], within) + dot3(across[yc], lower) + dot3(across[yc + 2], upper)
        )


OFFSETS = tuple(
    (a, b, c) for a in (-1, 0, 1) for b in (-1, 0, 1) for c in (-1, 0, 1) if (a, b, c) != (0, 0, 0)
)


def solve_kernel(
    own, other, coefs, wo, wz, from_prev_x, from_next_x, from_prev_y, from_next_y, facing_y, corners, pressure,
    solution, new_pressure, start, state, blocks, field,
):
    gx = lax.axis_index("gx")
    gy = lax.axis_index("gy")
    core = lax.axis_index("gz")
    size_x = lax.axis_size("gx")
    size_y = lax.axis_size("gy")

    at_x = iota((9, 128), 0) + gx - 4
    valid_x = (at_x >= 0) & (at_x < size_x)
    for yc in range(3):
        mine = own[pl.ds(16 * yc, 9), :] + other[pl.ds(48 + 16 * yc, 9), :]
        theirs = other[pl.ds(16 * yc, 9), :] + own[pl.ds(48 + 16 * yc, 9), :]
        valid = valid_x & (gy + yc - 1 >= 0) & (gy + yc - 1 < size_y)
        for zc in range(2):
            spot = (yc * 2 + zc) * 16
            base = zc * 688
            state[pl.ds(spot, 1), :] = coefs[pl.ds(base + yc, 1), :]
            state[pl.ds(spot + 1, 7), :] = coefs[pl.ds(base + 8 + yc * 32 + 26, 7, stride=96), :]
            state[pl.ds(spot + 8, 1), :] = coefs[pl.ds(base + 680 + yc, 1), :]
            value = jnp.where(core == zc, mine, theirs) * state[pl.ds(spot, 9), :]
            value = jnp.where(valid, value, 0.0)
            start[pl.ds(spot, 9), :] = value
            state[pl.ds(spot, 9), :] = value

    lane = iota((7, 128), 1)
    deep = lane % 32
    at_x = iota((7, 128), 0) + gx - 3
    valid_x = (at_x >= 0) & (at_x < size_x)
    for _ in range(3):
        totals = {}
        for yc in range(3):
            for zc in range(2):
                spot = (yc * 2 + zc) * 16 + 1
                totals[yc, zc] = (1.0 - damping) * state[pl.ds(spot, 7), :] + start[pl.ds(spot, 7), :]
        for a in (-1, 0, 1):
            shifted = {}
            for yc in range(3):
                low = state[pl.ds((yc * 2) * 16 + 1 + a, 7), :]
                high = state[pl.ds((yc * 2 + 1) * 16 + 1 + a, 7), :]
                shifted[yc, 0, 0] = low
                shifted[yc, 1, 0] = high
                shifted[yc, 0, 1] = jnp.where(deep == 31, pltpu.roll(high, 31, 1), pltpu.roll(low, 127, 1))
                shifted[yc, 1, 1] = jnp.where(deep == 31, 0.0, pltpu.roll(high, 127, 1))
                shifted[yc, 0, -1] = jnp.where(deep == 0, 0.0, pltpu.roll(low, 1, 1))
                shifted[yc, 1, -1] = jnp.where(deep == 0, pltpu.roll(low, 97, 1), pltpu.roll(high, 1, 1))
            for c in (-1, 0, 1):
                for zc in range(2):
                    up = [pltpu.roll(shifted[yc, zc, c], 96, 1) for yc in range(3)]
                    down = [pltpu.roll(shifted[yc, zc, c], 32, 1) for yc in range(3)]
                    zero = jnp.zeros((7, 128), F32)
                    for yc in range(3):
                        beyond = up[yc + 1] if yc < 2 else zero
                        behind = down[yc - 1] if yc > 0 else zero
                        values = {
                            -1: jnp.where(lane < 32, behind, down[yc]),
                            0: shifted[yc, zc, c],
                            1: jnp.where(lane >= 96, beyond, up[yc]),
                        }
                        for b in (-1, 0, 1):
                            if (a, b, c) == (0, 0, 0):
                                continue
                            number = OFFSETS.index((a, b, c))
                            coef = coefs[pl.ds(zc * 688 + 8 + yc * 32 + number, 7, stride=96), :]
                            totals[yc, zc] = totals[yc, zc] - coef * values[b]
        for yc in range(3):
            valid = valid_x & (gy + yc - 1 >= 0) & (gy + yc - 1 < size_y)
            for zc in range(2):
                state[pl.ds((yc * 2 + zc) * 16 + 1, 7), :] = jnp.where(valid, totals[yc, zc], 0.0)

    low = state[pl.ds(2 * 16 + 4, 1), :]
    high = state[pl.ds(3 * 16 + 4, 1), :]
    mine = jnp.where(core == 0, low, high)
    for by in range(4):
        moved = pltpu.roll(mine, (128 - 32 * by) % 128, 1) if by else mine
        solution[0, pl.ds(by, 1), :] = moved[:, 0:32]

    lane3 = iota((3, 128), 1)
    blocks[...] = jnp.zeros_like(blocks)
    for by in range(-1, 5):
        yc, at = (0, 3) if by < 0 else ((2, 0) if by > 3 else (1, by))
        low = state[pl.ds((yc * 2) * 16 + 3, 3), :]
        high = state[pl.ds((yc * 2 + 1) * 16 + 3, 3), :]
        low = pltpu.roll(low, (128 - 32 * at) % 128, 1) if at else low
        shift = (32 - 32 * at) % 128
        high = pltpu.roll(high, shift, 1) if shift else high
        blocks[pl.ds((by + 1) * 8, 3), :] = jnp.where(lane3 < 32, low, jnp.where(lane3 < 64, high, 0.0))
    inside, reach = spread(core)
    over_o = dot3(blocks[...], inside, NT)
    over_z = dot3(blocks[...], reach, NT)

    def factor(by, column):
        spot = (by + 1) * 8 + column
        return over_o[spot : spot + 1], over_z[spot : spot + 1]

    field[...] = jnp.zeros_like(field)
    for x in range(8):
        entries = [(None, 0, 0, 48, (x + 2) * 4, 1)]
        if x < 2:
            entries.append((from_prev_x, 0, 96, 8, x * 4, 0))
        if x >= 6:
            entries.append((from_next_x, 0, 96, 8, (x - 6) * 4, 2))
        carry = None
        for by in range(4):
            total8 = total4 = None
            for ref, base_o, base_z, step, begin, column in entries:
                factors = factor(by, column)
                for half in range(2):
                    w = ref if ref is not None else (wo, wz)[half]
                    first = (base_o, base_z)[half] + begin + by
                    term8 = w[pl.ds(first, 8, stride=step), :] * factors[half]
                    term4 = w[pl.ds(first + 8 * step, 4, stride=step), :] * factors[half]
                    total8 = term8 if total8 is None else total8 + term8
                    total4 = term4 if total4 is None else total4 + term4
            field[pl.ds(40 * x + 8 * by, 8), :] = total8
            if carry is not None:
                field[pl.ds(40 * x + 8 * by, 4), :] = total8[0:4] + carry
            carry = total4
        field[pl.ds(40 * x + 32, 4), :] = carry
    for side, (by, first_row, strip) in enumerate(((-1, 2, from_prev_y), (4, 32, from_next_y))):
        for n in range(2):
            middle = strip[pl.ds(2 * n * 12 + 2, 8), :] * factor(by, 1)[0]
            tile = faced(core, strip[pl.ds((2 * n + 1) * 12 + 2, 8), :], facing_y[pl.ds(side * 24 + n * 12 + 2, 8), :])
            middle = middle + tile * factor(by, 1)[1]
            rows = pl.ds(first_row + n, 8, stride=40)
            field[rows, :] = field[rows, :] + middle
            for column, first_x in ((0, 0), (2, 6)):
                spot = column * 8 + side * 8 + n * 4
                factors = factor(by, column)
                rows = pl.ds(40 * first_x + first_row + n, 2, stride=40)
                field[rows, :] = (
                    field[rows, :]
                    + corners[pl.ds(spot, 2), :] * factors[0]
                    + corners[pl.ds(spot + 2, 2), :] * factors[1]
                )
    for x in range(8):
        new_pressure[x] = pressure[x] + field[pl.ds(40 * x + 2, 32), :]


def call(kernel, out_shapes, scratch=(), **specs):
    single = not isinstance(out_shapes, (list, tuple))
    shapes = [out_shapes] if single else list(out_shapes)
    run = pl.pallas_call(
        kernel,
        out_shape=tuple(shapes) if not single else shapes[0],
        scratch_shapes=list(scratch),
        compiler_params=pltpu.CompilerParams(vmem_limit_bytes=24 * 1024 * 1024),
        **specs,
    )
    return run


def shape(*dims, dtype=F32):
    return jax.ShapeDtypeStruct(dims, dtype)


def shift(value, axis, steps):
    count = lax.axis_size(axis)
    return lax.ppermute(value, axis, [(i, (i + steps) % count) for i in range(count)])


def on_device(
    pressure, accumulation, trans_x, trans_y, trans_z, source, well_cells, well_rates, basis, coarse_off, coarse_diag
):
    wo, wz, to_next_y, to_prev_y, coarse = call(
        pack_kernel,
        [shape(576, 128), shape(576, 128), shape(96, 128), shape(88, 128), shape(32, 128)],
        [
            pltpu.VMEM((6, 576, 32), BF16),
            pltpu.VMEM((8, 32, 128), F32),
            pltpu.VMEM((8, 32, 128), F32),
            pltpu.VMEM((26, 1, 4, 32), F32),
            pltpu.VMEM((1, 4, 32), F32),
            pltpu.SemaphoreType.DMA((5,)),
        ],
        in_specs=[pl.BlockSpec(memory_space=pltpu.HBM)] * 5,
    )(
        *(
            pltpu.with_memory_space_constraint(operand, pltpu.HBM)
            for operand in (basis.reshape(6, 576, 32), pressure, trans_y, coarse_off, coarse_diag)
        )
    )
    from_prev_y = shift(to_next_y, "gy", 1)
    from_next_y = shift(to_prev_y, "gy", -1)
    facing = shift(wz, "gz", 1)
    facing_p = shift(pressure, "gz", 1)
    facing_t = shift(trans_z, "gz", 1)
    wz, to_next_x, to_prev_x, strips = call(
        relay_kernel, [shape(576, 128), shape(368, 128), shape(336, 128), shape(48, 128)]
    )(wo, wz, facing, pressure, trans_x, coarse, from_prev_y, from_next_y)
    from_prev_x = shift(to_next_x, "gx", 1)
    from_next_x = shift(to_prev_x, "gx", -1)
    facing_y = shift(strips, "gz", 1)

    corners, up, down = call(collect_kernel, [shape(32, 128), shape(224, 128, dtype=BF16), shape(224, 128, dtype=BF16)])(
        from_prev_x, from_next_x, to_next_x
    )
    facing_x = shift(corners, "gz", 1)
    wells = call(wells_kernel, shape(256, 128))(well_cells.reshape(8, 128), well_rates.reshape(8, 128))
    partial = call(local_kernel, shape(8, 32, 128))(
        pressure, accumulation, trans_x, trans_y, trans_z, source, wells, facing_p, facing_t, from_prev_y, from_next_y
    )
    residual, field, sums_o, sums_z = call(
        sums_kernel, [shape(8, 32, 128), shape(320, 128), shape(48, 128), shape(48, 128)]
    )(partial, pressure, trans_x, wo, wz, from_prev_x, from_next_x, from_prev_y, from_next_y, facing_y)
    count = lax.axis_size("gx") * lax.axis_size("gy")
    message, corners = call(
        tail_kernel,
        [shape(5 * count, 128), shape(32, 128)],
        [pltpu.VMEM((48, 128), F32), pltpu.VMEM((48, 128), F32), pltpu.VMEM((40, 128), F32)],
    )(field, sums_o, sums_z, corners, facing_x)
    shared = lax.all_to_all(message.reshape(count, 1, 640), ("gx", "gy"), 0, 0)
    shared = shared.reshape(5 * count, 128)

    near = call(window_kernel, shape(688, 128))(
        shift(up, "gx", 3), shift(down, "gx", -3), from_prev_x, to_next_x, from_next_x
    )
    coefs = call(stack_kernel, shape(1376, 128))(near, shift(near, "gz", 1))

    own = call(gather_kernel, shape(96, 128), [pltpu.VMEM((26 * 60, 128), F32)])(shared)
    other = shift(own, "gz", 1)
    solution, new_pressure = call(
        solve_kernel,
        [shape(1, 4, 32), shape(8, 32, 128)],
        [
            pltpu.VMEM((96, 128), F32),
            pltpu.VMEM((96, 128), F32),
            pltpu.VMEM((48, 128), F32),
            pltpu.VMEM((320, 128), F32),
        ],
    )(own, other, coefs, wo, wz, from_prev_x, from_next_x, from_prev_y, from_next_y, facing_y, corners, pressure)
    return residual, solution, new_pressure


def solution(mesh):
    cells = P("gx", "gy", "gz")
    in_specs = (
        cells, cells, cells, cells, cells, cells, P(), P(),
        P(None, None, None, "gx", "gy", "gz"), P(None, "gx", "gy", "gz"), cells,
    )

    return jax.shard_map(on_device, mesh=mesh, in_specs=in_specs, out_specs=(cells, cells, cells), check_vma=False)
```

profile of v0, /device:TPU:1, one launch (start us, length us, event | category | flops | bytes accessed | tf_op | source)
XLA Modules:
  0.0 66.1 jit_solution(6077738602063538982)
XLA Ops:
  0.6 0.0 copy-start
  0.6 0.0 copy-start.1
  0.7 1.8 %shard_map.131 = (f32[576,128]{1,0:T(8,128)S(1)}, f32[576,128]{1,0:T(8,128)S(1)}, f32[96,128]{1,0:T(8,128)S(1)}, f32[88,128]{1,0:T(8,128)S(1)}, f32[32,128]{1,0:T(8,128)S(1)}) custom-call(bf16[6,576,32]{2,1,0:T(8,128)(2,1)} %bitcast.8, f32[8,32,128]{2,1,0:T(8,128)} %pressure.7, f32[8,32,128]{2,1,0:T(8,128)} %trans_y.1, f32[26,1,4,32]{3,2,1,0:T(4,128)} %coarse_off_in.1, ...), custom_call_target="tpu_custom_call" | custom-call | tf_op jit(solution)/shard_map/pallas_call | solution.py:558
  2.5 3.3 %collective-permute-start.4 = (f32[576,128]{1,0:T(8,128)S(1)}, f32[576,128]{1,0:T(8,128)S(1)}, u32[]{:S(2)}, u32[]{:S(2)}) collective-permute-start(f32[576,128]{1,0:T(8,128)S(1)} %get-tuple-element.26.wz), channel_id=1, source_target_pairs={{0,1},{1,0},{2,3},{3,2},{4,5},{5,4},{6,7},{7,6},{8,9},{9,8},{10,11... | collective-permute-start | bytes 884744 | tf_op jit(solution)/shard_map/ppermute | solution.py:552
  5.8 5.2 %collective-permute-start.2 = (f32[96,128]{1,0:T(8,128)S(1)}, f32[96,128]{1,0:T(8,128)S(1)}, u32[]{:S(2)}, u32[]{:S(2)}) collective-permute-start(f32[96,128]{1,0:T(8,128)S(1)} %get-tuple-element.23), channel_id=1, source_target_pairs={{0,2},{2,4},{4,6},{6,8},{8,10},{10,12},{12,14},{14,0},{1,3},{3,5},... | collective-permute-start | bytes 147464 | tf_op jit(solution)/shard_map/ppermute | solution.py:552
  11.0 2.5 %collective-permute-start.3 = (f32[88,128]{1,0:T(8,128)S(1)}, f32[88,128]{1,0:T(8,128)S(1)}, u32[]{:S(2)}, u32[]{:S(2)}) collective-permute-start(f32[88,128]{1,0:T(8,128)S(1)} %get-tuple-element.24), channel_id=1, source_target_pairs={{0,14},{2,0},{4,2},{6,4},{8,6},{10,8},{12,10},{14,12},{1,15},{3,1}... | collective-permute-start | bytes 135176 | tf_op jit(solution)/shard_map/ppermute | solution.py:552
  13.4 4.5 %collective-permute-done.3.from_next_y = f32[88,128]{1,0:T(8,128)S(1)} collective-permute-done((f32[88,128]{1,0:T(8,128)S(1)}, f32[88,128]{1,0:T(8,128)S(1)}, u32[]{:S(2)}, u32[]{:S(2)}) %collective-permute-start.3) | collective-permute-done | bytes 45088 | tf_op jit(solution)/shard_map/ppermute | solution.py:552
  17.9 0.0 collective-permute-done.2.from_prev_y
  17.9 0.0 collective-permute-done.4.facing
  17.9 0.0 copy-done
  17.9 0.0 copy-done.1
  17.9 0.0 copy-start.4
  17.9 0.2 shard_map.133
  18.1 1.3 %collective-permute-start.5 = (f32[368,128]{1,0:T(8,128)S(1)}, f32[368,128]{1,0:T(8,128)S(1)}, u32[]{:S(2)}, u32[]{:S(2)}) collective-permute-start(f32[368,128]{1,0:T(8,128)S(1)} %get-tuple-element.29.own), channel_id=1, source_target_pairs={{0,16},{16,32},{32,48},{48,64},{64,80},{80,96},{96,112},{112,128},... | collective-permute-start | bytes 565256 | tf_op jit(solution)/shard_map/ppermute | solution.py:552
  19.3 4.2 %collective-permute-start.6 = (f32[336,128]{1,0:T(8,128)S(1)}, f32[336,128]{1,0:T(8,128)S(1)}, u32[]{:S(2)}, u32[]{:S(2)}) collective-permute-start(f32[336,128]{1,0:T(8,128)S(1)} %get-tuple-element.30), channel_id=1, source_target_pairs={{0,240},{16,0},{32,16},{48,32},{64,48},{80,64},{96,80},{112,96},{1... | collective-permute-start | bytes 516104 | tf_op jit(solution)/shard_map/ppermute | solution.py:552
  23.5 2.0 %collective-permute-start = (f32[8,32,128]{2,1,0:T(8,128)S(1)}, f32[8,32,128]{2,1,0:T(8,128)S(1)}, u32[]{:S(2)}, u32[]{:S(2)}) collective-permute-start(f32[8,32,128]{2,1,0:T(8,128)S(1)} %copy-done), channel_id=1, source_target_pairs={{0,1},{1,0},{2,3},{3,2},{4,5},{5,4},{6,7},{7,6},{8,9},{9,8},{10,11... | collective-permute-start | bytes 393224 | tf_op jit(solution)/shard_map/ppermute | solution.py:552
  25.5 0.0 copy-done.4
  25.5 0.0 collective-permute-start.1
  25.5 0.5 collective-permute-start.7
  26.0 0.0 collective-permute-done.6.from_next_x
  26.0 0.9 %collective-permute-done.5.from_prev_x = f32[368,128]{1,0:T(8,128)S(1)} collective-permute-done((f32[368,128]{1,0:T(8,128)S(1)}, f32[368,128]{1,0:T(8,128)S(1)}, u32[]{:S(2)}, u32[]{:S(2)}) %collective-permute-start.5) | collective-permute-done | bytes 188448 | tf_op jit(solution)/shard_map/ppermute | solution.py:552
  26.9 0.0 copy-start.2
  26.9 2.4 %collective-permute-start.8 = (f32[32,128]{1,0:T(8,128)S(1)}, f32[32,128]{1,0:T(8,128)S(1)}, u32[]{:S(2)}, u32[]{:S(2)}) collective-permute-start(f32[32,128]{1,0:T(8,128)S(1)} %get-tuple-element.36.corners), channel_id=1, source_target_pairs={{0,1},{1,0},{2,3},{3,2},{4,5},{5,4},{6,7},{7,6},{8,9},{9,8},{10,11... | collective-permute-start | bytes 49160 | tf_op jit(solution)/shard_map/ppermute | solution.py:552
  29.3 0.0 copy-done.6
  29.3 0.6 shard_map.130.wells
  29.9 0.0 collective-permute-done.facing_p
  29.9 0.0 collective-permute-done.1.facing_t
  29.9 0.0 copy-done.3
  29.9 0.0 copy-done.5
  30.0 0.0 copy-done.2
  30.0 0.3 shard_map.132.partial
  30.3 0.0 collective-permute-done.7.facing_y
  30.3 0.8 %shard_map.134 = (f32[8,32,128]{2,1,0:T(8,128)}, f32[320,128]{1,0:T(8,128)S(1)}, f32[48,128]{1,0:T(8,128)S(1)}, f32[48,128]{1,0:T(8,128)S(1)}) custom-call(f32[8,32,128]{2,1,0:T(8,128)S(1)} %shard_map.132.partial, f32[8,32,128]{2,1,0:T(8,128)S(1)} %copy-done, f32[8,32,128]{2,1,0:T(8,128)S(1)} %copy-done.1, f32[576,128]{1,0:T(8,128)S(1)} %get-tuple-element.25.wo, ...), custom_call_target="tpu_custom_call" | custom-call | tf_op jit(solution)/shard_map/pallas_call | solution.py:596
  31.1 0.0 collective-permute-done.8.facing_x
  31.1 1.1 %shard_map.136 = (f32[640,128]{1,0:T(8,128)}, f32[32,128]{1,0:T(8,128)S(1)}) custom-call(f32[320,128]{1,0:T(8,128)S(1)} %get-tuple-element.33.field, f32[48,128]{1,0:T(8,128)S(1)} %get-tuple-element.34.sums_o, f32[48,128]{1,0:T(8,128)S(1)} %get-tuple-element.35.sums_z, f32[32,128]{1,0:T(8,128)S(1)} %get-tuple-element.36.corners, ...), custom_call_target="tpu_custom_call" | custom-call | tf_op jit(solution)/shard_map/pallas_call | solution.py:600
  32.2 12.4 %all-to-all-start = ((f32[128,1,640]{2,1,0:T(1,128)}), f32[128,1,640]{2,1,0:T(1,128)S(1)}, u32[]{:S(2)}, u32[]{:S(2)}) async-start(f32[128,1,640]{2,1,0:T(1,128)} %bitcast.3), calls=%async_computation | async-start | bytes 655360 | tf_op jit(solution)/shard_map/all_to_all | solution.py:605
  44.6 1.9 %collective-permute-start.10 = (bf16[224,128]{1,0:T(8,128)(2,1)S(1)}, bf16[224,128]{1,0:T(8,128)(2,1)S(1)}, u32[]{:S(2)}, u32[]{:S(2)}) collective-permute-start(bf16[224,128]{1,0:T(8,128)(2,1)S(1)} %get-tuple-element.38), channel_id=1, source_target_pairs={{0,48},{16,64},{32,80},{48,96},{64,112},{80,128},{96,144},{112,160... | collective-permute-start | bytes 172040 | tf_op jit(solution)/shard_map/ppermute | solution.py:552
  46.6 2.3 %collective-permute-start.11 = (bf16[224,128]{1,0:T(8,128)(2,1)S(1)}, bf16[224,128]{1,0:T(8,128)(2,1)S(1)}, u32[]{:S(2)}, u32[]{:S(2)}) collective-permute-start(bf16[224,128]{1,0:T(8,128)(2,1)S(1)} %get-tuple-element.39), channel_id=1, source_target_pairs={{0,208},{16,224},{32,240},{48,0},{64,16},{80,32},{96,48},{112,64},... | collective-permute-start | bytes 172040 | tf_op jit(solution)/shard_map/ppermute | solution.py:552
  48.9 5.7 %collective-permute-done.10.up = bf16[224,128]{1,0:T(8,128)(2,1)S(1)} collective-permute-done((bf16[224,128]{1,0:T(8,128)(2,1)S(1)}, bf16[224,128]{1,0:T(8,128)(2,1)S(1)}, u32[]{:S(2)}, u32[]{:S(2)}) %collective-permute-start.10) | collective-permute-done | bytes 57376 | tf_op jit(solution)/shard_map/ppermute | solution.py:552
  54.5 0.0 collective-permute-done.11.down
  54.6 3.7 %collective-permute-start.12 = (f32[688,128]{1,0:T(8,128)S(1)}, f32[688,128]{1,0:T(8,128)S(1)}, u32[]{:S(2)}, u32[]{:S(2)}) collective-permute-start(f32[688,128]{1,0:T(8,128)S(1)} %shard_map.138.near), channel_id=1, source_target_pairs={{0,1},{1,0},{2,3},{3,2},{4,5},{5,4},{6,7},{7,6},{8,9},{9,8},{10,11... | collective-permute-start | bytes 1056776 | tf_op jit(solution)/shard_map/ppermute | solution.py:552
  58.3 0.0 all-to-all-done
  58.3 0.4 shard_map.137.own
  58.7 4.1 %collective-permute-start.9 = (f32[96,128]{1,0:T(8,128)S(1)}, f32[96,128]{1,0:T(8,128)S(1)}, u32[]{:S(2)}, u32[]{:S(2)}) collective-permute-start(f32[96,128]{1,0:T(8,128)S(1)} %shard_map.137.own), channel_id=1, source_target_pairs={{0,1},{1,0},{2,3},{3,2},{4,5},{5,4},{6,7},{7,6},{8,9},{9,8},{10,11... | collective-permute-start | bytes 147464 | tf_op jit(solution)/shard_map/ppermute | solution.py:552
  62.8 0.0 collective-permute-done.12.far
  62.8 0.1 shard_map.139.coefs
  62.8 0.8 %collective-permute-done.9.other = f32[96,128]{1,0:T(8,128)S(1)} collective-permute-done((f32[96,128]{1,0:T(8,128)S(1)}, f32[96,128]{1,0:T(8,128)S(1)}, u32[]{:S(2)}, u32[]{:S(2)}) %collective-permute-start.9) | collective-permute-done | bytes 49184 | tf_op jit(solution)/shard_map/ppermute | solution.py:552
  63.7 2.4 %shard_map.140 = (f32[1,4,32]{2,1,0:T(4,128)}, f32[8,32,128]{2,1,0:T(8,128)}) custom-call(f32[96,128]{1,0:T(8,128)S(1)} %shard_map.137.own, f32[96,128]{1,0:T(8,128)S(1)} %collective-permute-done.9.other, f32[1376,128]{1,0:T(8,128)S(1)} %shard_map.139.coefs, f32[576,128]{1,0:T(8,128)S(1)} %get-tuple-element.25.wo, f32[576,128]{1,0:T(8,128)S(1)} %get-tuple-element.28.wz, ...), custom_call_target="tpu_custom_call" | custom-call | tf_op jit(solution)/shard_map/pallas_call | solution.py:615
  (7 shorter events, 0.1 us)
Async XLA Ops:
  0.6 17.2 %copy-start = (f32[8,32,128]{2,1,0:T(8,128)S(1)}, f32[8,32,128]{2,1,0:T(8,128)}, u32[]{:S(2)}) copy-start(f32[8,32,128]{2,1,0:T(8,128)} %pressure.7) | copy-start | bytes 393220
  0.6 17.2 %copy-start.1 = (f32[8,32,128]{2,1,0:T(8,128)S(1)}, f32[8,32,128]{2,1,0:T(8,128)}, u32[]{:S(2)}) copy-start(f32[8,32,128]{2,1,0:T(8,128)} %trans_x.5) | copy-start | bytes 393220
  2.5 15.4 %collective-permute-start.4 = (f32[576,128]{1,0:T(8,128)S(1)}, f32[576,128]{1,0:T(8,128)S(1)}, u32[]{:S(2)}, u32[]{:S(2)}) collective-permute-start(f32[576,128]{1,0:T(8,128)S(1)} %get-tuple-element.26.wz), channel_id=1, source_target_pairs={{0,1},{1,0},{2,3},{3,2},{4,5},{5,4},{6,7},{7,6},{8,9},{9,8},{10,11... | collective-permute-start | bytes 884744 | tf_op jit(solution)/shard_map/ppermute | solution.py:552
  5.8 12.1 %collective-permute-start.2 = (f32[96,128]{1,0:T(8,128)S(1)}, f32[96,128]{1,0:T(8,128)S(1)}, u32[]{:S(2)}, u32[]{:S(2)}) collective-permute-start(f32[96,128]{1,0:T(8,128)S(1)} %get-tuple-element.23), channel_id=1, source_target_pairs={{0,2},{2,4},{4,6},{6,8},{8,10},{10,12},{12,14},{14,0},{1,3},{3,5},... | collective-permute-start | bytes 147464 | tf_op jit(solution)/shard_map/ppermute | solution.py:552
  11.0 6.9 %collective-permute-start.3 = (f32[88,128]{1,0:T(8,128)S(1)}, f32[88,128]{1,0:T(8,128)S(1)}, u32[]{:S(2)}, u32[]{:S(2)}) collective-permute-start(f32[88,128]{1,0:T(8,128)S(1)} %get-tuple-element.24), channel_id=1, source_target_pairs={{0,14},{2,0},{4,2},{6,4},{8,6},{10,8},{12,10},{14,12},{1,15},{3,1}... | collective-permute-start | bytes 135176 | tf_op jit(solution)/shard_map/ppermute | solution.py:552
  17.9 7.6 %copy-start.4 = (f32[8,32,128]{2,1,0:T(8,128)S(1)}, f32[8,32,128]{2,1,0:T(8,128)}, u32[]{:S(2)}) copy-start(f32[8,32,128]{2,1,0:T(8,128)} %trans_z.1) | copy-start | bytes 393220
  18.1 8.8 %collective-permute-start.5 = (f32[368,128]{1,0:T(8,128)S(1)}, f32[368,128]{1,0:T(8,128)S(1)}, u32[]{:S(2)}, u32[]{:S(2)}) collective-permute-start(f32[368,128]{1,0:T(8,128)S(1)} %get-tuple-element.29.own), channel_id=1, source_target_pairs={{0,16},{16,32},{32,48},{48,64},{64,80},{80,96},{96,112},{112,128},... | collective-permute-start | bytes 565256 | tf_op jit(solution)/shard_map/ppermute | solution.py:552
  19.3 6.7 %collective-permute-start.6 = (f32[336,128]{1,0:T(8,128)S(1)}, f32[336,128]{1,0:T(8,128)S(1)}, u32[]{:S(2)}, u32[]{:S(2)}) collective-permute-start(f32[336,128]{1,0:T(8,128)S(1)} %get-tuple-element.30), channel_id=1, source_target_pairs={{0,240},{16,0},{32,16},{48,32},{64,48},{80,64},{96,80},{112,96},{1... | collective-permute-start | bytes 516104 | tf_op jit(solution)/shard_map/ppermute | solution.py:552
  23.5 6.4 %collective-permute-start = (f32[8,32,128]{2,1,0:T(8,128)S(1)}, f32[8,32,128]{2,1,0:T(8,128)S(1)}, u32[]{:S(2)}, u32[]{:S(2)}) collective-permute-start(f32[8,32,128]{2,1,0:T(8,128)S(1)} %copy-done), channel_id=1, source_target_pairs={{0,1},{1,0},{2,3},{3,2},{4,5},{5,4},{6,7},{7,6},{8,9},{9,8},{10,11... | collective-permute-start | bytes 393224 | tf_op jit(solution)/shard_map/ppermute | solution.py:552
  25.5 4.4 %collective-permute-start.1 = (f32[8,32,128]{2,1,0:T(8,128)S(1)}, f32[8,32,128]{2,1,0:T(8,128)S(1)}, u32[]{:S(2)}, u32[]{:S(2)}) collective-permute-start(f32[8,32,128]{2,1,0:T(8,128)S(1)} %copy-done.4), channel_id=1, source_target_pairs={{0,1},{1,0},{2,3},{3,2},{4,5},{5,4},{6,7},{7,6},{8,9},{9,8},{10,11... | collective-permute-start | bytes 393224 | tf_op jit(solution)/shard_map/ppermute | solution.py:552
  25.5 4.8 %collective-permute-start.7 = (f32[48,128]{1,0:T(8,128)S(1)}, f32[48,128]{1,0:T(8,128)S(1)}, u32[]{:S(2)}, u32[]{:S(2)}) collective-permute-start(f32[48,128]{1,0:T(8,128)S(1)} %get-tuple-element.31), channel_id=1, source_target_pairs={{0,1},{1,0},{2,3},{3,2},{4,5},{5,4},{6,7},{7,6},{8,9},{9,8},{10,11... | collective-permute-start | bytes 73736 | tf_op jit(solution)/shard_map/ppermute | solution.py:552
  26.9 2.4 %copy-start.6 = (s32[1024]{0:T(1024)S(1)}, s32[1024]{0:T(1024)}, u32[]{:S(2)}) copy-start(s32[1024]{0:T(1024)} %param.17) | copy-start | bytes 12292
  26.9 2.4 %copy-start.7 = (f32[1024]{0:T(1024)S(1)}, f32[1024]{0:T(1024)}, u32[]{:S(2)}) copy-start(f32[1024]{0:T(1024)} %param.18) | copy-start | bytes 12292
  26.9 3.0 %copy-start.3 = (f32[8,32,128]{2,1,0:T(8,128)S(1)}, f32[8,32,128]{2,1,0:T(8,128)}, u32[]{:S(2)}) copy-start(f32[8,32,128]{2,1,0:T(8,128)} %accumulation.1) | copy-start | bytes 393220
  26.9 3.1 %copy-start.5 = (f32[8,32,128]{2,1,0:T(8,128)S(1)}, f32[8,32,128]{2,1,0:T(8,128)}, u32[]{:S(2)}) copy-start(f32[8,32,128]{2,1,0:T(8,128)} %source.1) | copy-start | bytes 393220
  26.9 3.0 %copy-start.2 = (f32[8,32,128]{2,1,0:T(8,128)S(1)}, f32[8,32,128]{2,1,0:T(8,128)}, u32[]{:S(2)}) copy-start(f32[8,32,128]{2,1,0:T(8,128)} %trans_y.1) | copy-start | bytes 393220
  26.9 4.2 %collective-permute-start.8 = (f32[32,128]{1,0:T(8,128)S(1)}, f32[32,128]{1,0:T(8,128)S(1)}, u32[]{:S(2)}, u32[]{:S(2)}) collective-permute-start(f32[32,128]{1,0:T(8,128)S(1)} %get-tuple-element.36.corners), channel_id=1, source_target_pairs={{0,1},{1,0},{2,3},{3,2},{4,5},{5,4},{6,7},{7,6},{8,9},{9,8},{10,11... | collective-permute-start | bytes 49160 | tf_op jit(solution)/shard_map/ppermute | solution.py:552
  32.2 26.0 %all-to-all-start = ((f32[128,1,640]{2,1,0:T(1,128)}), f32[128,1,640]{2,1,0:T(1,128)S(1)}, u32[]{:S(2)}, u32[]{:S(2)}) async-start(f32[128,1,640]{2,1,0:T(1,128)} %bitcast.3), calls=%async_computation | async-start | bytes 655360 | tf_op jit(solution)/shard_map/all_to_all | solution.py:605
  44.6 9.9 %collective-permute-start.10 = (bf16[224,128]{1,0:T(8,128)(2,1)S(1)}, bf16[224,128]{1,0:T(8,128)(2,1)S(1)}, u32[]{:S(2)}, u32[]{:S(2)}) collective-permute-start(bf16[224,128]{1,0:T(8,128)(2,1)S(1)} %get-tuple-element.38), channel_id=1, source_target_pairs={{0,48},{16,64},{32,80},{48,96},{64,112},{80,128},{96,144},{112,160... | collective-permute-start | bytes 172040 | tf_op jit(solution)/shard_map/ppermute | solution.py:552
  46.6 8.0 %collective-permute-start.11 = (bf16[224,128]{1,0:T(8,128)(2,1)S(1)}, bf16[224,128]{1,0:T(8,128)(2,1)S(1)}, u32[]{:S(2)}, u32[]{:S(2)}) collective-permute-start(bf16[224,128]{1,0:T(8,128)(2,1)S(1)} %get-tuple-element.39), channel_id=1, source_target_pairs={{0,208},{16,224},{32,240},{48,0},{64,16},{80,32},{96,48},{112,64},... | collective-permute-start | bytes 172040 | tf_op jit(solution)/shard_map/ppermute | solution.py:552
  54.6 8.2 %collective-permute-start.12 = (f32[688,128]{1,0:T(8,128)S(1)}, f32[688,128]{1,0:T(8,128)S(1)}, u32[]{:S(2)}, u32[]{:S(2)}) collective-permute-start(f32[688,128]{1,0:T(8,128)S(1)} %shard_map.138.near), channel_id=1, source_target_pairs={{0,1},{1,0},{2,3},{3,2},{4,5},{5,4},{6,7},{7,6},{8,9},{9,8},{10,11... | collective-permute-start | bytes 1056776 | tf_op jit(solution)/shard_map/ppermute | solution.py:552
  58.7 4.9 %collective-permute-start.9 = (f32[96,128]{1,0:T(8,128)S(1)}, f32[96,128]{1,0:T(8,128)S(1)}, u32[]{:S(2)}, u32[]{:S(2)}) collective-permute-start(f32[96,128]{1,0:T(8,128)S(1)} %shard_map.137.own), channel_id=1, source_target_pairs={{0,1},{1,0},{2,3},{3,2},{4,5},{5,4},{6,7},{7,6},{8,9},{9,8},{10,11... | collective-permute-start | bytes 147464 | tf_op jit(solution)/shard_map/ppermute | solution.py:552
where the time goes:
time: 66.3 us; the launch traced here: 66.1 us
  starting transfers between devices  45.7 us (69%)
  waiting for transfers between devices  11.8 us (18%)
  Pallas kernels  7.74 us (12%)
  between operations  0.79 us (1%)
    ppermute x13, starting transfers between devices, shift(): lax.ppermute(value, axis, [(i, (i + steps) % count) for i in range(count)])  33.3 us
    all_to_all x1, starting transfers between devices, on_device(): shared = lax.all_to_all(message.reshape(count, 1, 640), ('gx', 'gy'), 0, 0)  12.4 us
    ppermute x13, waiting for transfers between devices, shift(): lax.ppermute(value, axis, [(i, (i + steps) % count) for i in range(count)])  11.8 us
    pallas_call x1, Pallas kernels, on_device(): call(solve_kernel, [shape(1, 4, 32), shape(8, 32, 128)], [pltpu.VMEM((96,...  2.41 us
    pallas_call x1, Pallas kernels, on_device(): call(pack_kernel, [shape(576, 128), shape(576, 128), shape(96, 128), shap...  1.81 us
  transfers between devices with their start and end apart: 14, of which 4 were waited for; matrix products, arithmetic and copies ran while one was open for 0% of the time, Pallas kernels for 3%

commit v1 on v0

--- a/solution.py
+++ b/solution.py
@@ -110,31 +110,38 @@
     to_prev_y[pl.ds(56, 32), :] = coarse[...]
 
 
-def relay_kernel(wo, wz, facing, pressure, trans_x, coarse, from_prev_y, from_next_y, whole, to_next_x, to_prev_x, strips):
-    core = lax.axis_index("gz")
+def relay_kernel(
+    wo, wz, facing, partial, pressure, trans_x, coarse, from_prev_y, from_next_y,
+    whole, near_next, near_prev, to_next_x, to_prev_x, strips,
+):
+    core = lax.axis_index("gz")
+    near_next[pl.ds(0, 32), :] = pressure[7]
+    near_next[pl.ds(32, 32), :] = trans_x[7]
+    near_next[pl.ds(64, 32), :] = partial[6]
+    near_next[pl.ds(96, 32), :] = partial[7]
+    near_prev[pl.ds(0, 32), :] = pressure[0]
+    near_prev[pl.ds(32, 32), :] = partial[0]
+    near_prev[pl.ds(64, 32), :] = partial[1]
     whole[...] = faced(core, wz[...], facing[...])
     for j in range(12):
         for half, w in enumerate((wo, whole)):
             to_next_x[pl.ds(96 * half + 8 * j, 8), :] = w[pl.ds(48 * j + 40, 8), :]
             to_prev_x[pl.ds(96 * half + 8 * j, 8), :] = w[pl.ds(48 * j, 8), :]
-    to_next_x[pl.ds(192, 32), :] = pressure[7]
-    to_prev_x[pl.ds(192, 32), :] = pressure[0]
     for side, strip in enumerate((from_prev_y, from_next_y)):
         for n in range(2):
             strips[pl.ds(side * 24 + n * 12, 12), :] = strip[pl.ds((2 * n + 1) * 12, 12), :]
         for spot in range(4):
-            to_next_x[pl.ds(224 + side * 8 + spot * 2, 2), :] = strip[pl.ds(spot * 12 + 10, 2), :]
-            to_prev_x[pl.ds(224 + side * 8 + spot * 2, 2), :] = strip[pl.ds(spot * 12, 2), :]
+            to_next_x[pl.ds(192 + side * 8 + spot * 2, 2), :] = strip[pl.ds(spot * 12 + 10, 2), :]
+            to_prev_x[pl.ds(192 + side * 8 + spot * 2, 2), :] = strip[pl.ds(spot * 12, 2), :]
     for ref in (to_next_x, to_prev_x):
-        ref[pl.ds(240, 32), :] = from_prev_y[pl.ds(64, 32), :]
-        ref[pl.ds(272, 32), :] = coarse[...]
-        ref[pl.ds(304, 32), :] = from_next_y[pl.ds(56, 32), :]
-    to_next_x[pl.ds(336, 32), :] = trans_x[7]
+        ref[pl.ds(208, 32), :] = from_prev_y[pl.ds(64, 32), :]
+        ref[pl.ds(240, 32), :] = coarse[...]
+        ref[pl.ds(272, 32), :] = from_next_y[pl.ds(56, 32), :]
 
 
 def collect_kernel(from_prev_x, from_next_x, own, corners, up, down):
-    corners[pl.ds(0, 16), :] = from_prev_x[pl.ds(224, 16), :]
-    corners[pl.ds(16, 16), :] = from_next_x[pl.ds(224, 16), :]
+    corners[pl.ds(0, 16), :] = from_prev_x[pl.ds(192, 16), :]
+    corners[pl.ds(16, 16), :] = from_next_x[pl.ds(192, 16), :]
     at = iota((96, 128), 0) % 32
 
     def narrow(rows):
@@ -142,11 +149,11 @@
         return jnp.where(at == 27, pltpu.roll(rest, 1, 0), rows).astype(BF16)
 
     for ref, far, near in ((up, from_prev_x, from_next_x), (down, from_next_x, from_prev_x)):
-        outer = narrow(far[pl.ds(240, 96), :]).astype(F32)
+        outer = narrow(far[pl.ds(208, 96), :]).astype(F32)
         inverses = [outer[32 * yc + 24 : 32 * yc + 32] for yc in range(3)]
         ref[pl.ds(0, 32), :] = jnp.concatenate(inverses + [jnp.zeros((8, 128), F32)], axis=0).astype(BF16)
-        ref[pl.ds(32, 96), :] = narrow(own[pl.ds(240, 96), :])
-        ref[pl.ds(128, 96), :] = narrow(near[pl.ds(240, 96), :])
+        ref[pl.ds(32, 96), :] = narrow(own[pl.ds(208, 96), :])
+        ref[pl.ds(128, 96), :] = narrow(near[pl.ds(208, 96), :])
 
 
 def window_kernel(up, down, from_prev_x, own, from_next_x, near):
@@ -162,9 +169,9 @@
             near[pl.ds(spot + yc, 1), :] = outer[8 * yc + 2 : 8 * yc + 3] + outer[8 * yc + 3 : 8 * yc + 4]
     near[pl.ds(8, 96), :] = wide(up[pl.ds(32, 96), :])
     near[pl.ds(104, 96), :] = wide(up[pl.ds(128, 96), :])
-    near[pl.ds(200, 96), :] = from_prev_x[pl.ds(240, 96), :]
-    near[pl.ds(296, 96), :] = own[pl.ds(240, 96), :]
-    near[pl.ds(392, 96), :] = from_next_x[pl.ds(240, 96), :]
+    near[pl.ds(200, 96), :] = from_prev_x[pl.ds(208, 96), :]
+    near[pl.ds(296, 96), :] = own[pl.ds(208, 96), :]
+    near[pl.ds(392, 96), :] = from_next_x[pl.ds(208, 96), :]
     near[pl.ds(488, 96), :] = wide(down[pl.ds(128, 96), :])
     near[pl.ds(584, 96), :] = wide(down[pl.ds(32, 96), :])
 
@@ -230,117 +237,88 @@
 
 
 def sums_kernel(
-    partial, pressure, trans_x, wo, wz, from_prev_x, from_next_x, from_prev_y, from_next_y, facing_y,
-    residual, field, sums_o, sums_z,
+    partial, pressure, trans_x, wo, wz, near_from_prev, near_from_next, from_prev_y, from_next_y, facing_y,
+    residual, message, field, sums_o, sums_z,
 ):
     gx = lax.axis_index("gx")
     core = lax.axis_index("gz")
     size_x = lax.axis_size("gx")
     has_next_x = jnp.where(gx < size_x - 1, 1.0, 0.0)
     has_prev_x = jnp.where(gx > 0, 1.0, 0.0)
-    field[...] = jnp.zeros_like(field)
+    p_prev = near_from_prev[pl.ds(0, 32), :] * has_prev_x
+    t_prev = near_from_prev[pl.ds(32, 32), :] * has_prev_x
+    p_next = near_from_next[pl.ds(0, 32), :] * has_next_x
+    flux_prev = t_prev * (pressure[0] - p_prev)
+    flux_next = trans_x[7] * (pressure[7] - p_next)
+    planes = [
+        near_from_prev[pl.ds(64, 32), :] * has_prev_x,
+        near_from_prev[pl.ds(96, 32), :] * has_prev_x + flux_prev * has_prev_x,
+    ]
     for x in range(8):
         value = partial[x]
-        here = pressure[x]
         if x == 0:
-            value = value - from_prev_x[pl.ds(336, 32), :] * has_prev_x * (
-                here - from_prev_x[pl.ds(192, 32), :] * has_prev_x
-            )
+            value = value - flux_prev
         if x == 7:
-            value = value - trans_x[7] * (here - from_next_x[pl.ds(192, 32), :] * has_next_x)
+            value = value - flux_next
         residual[x] = value
-        field[pl.ds(40 * x + 2, 32), :] = value
+        planes.append(value)
+    planes.append(near_from_next[pl.ds(32, 32), :] * has_next_x + flux_next * has_next_x)
+    planes.append(near_from_next[pl.ds(64, 32), :] * has_next_x)
+    field[...] = jnp.zeros_like(field)
+    for i, plane in enumerate(planes):
+        field[pl.ds(40 * i + 2, 32), :] = plane
+
     sums_o[...] = jnp.zeros_like(sums_o)
     sums_z[...] = jnp.zeros_like(sums_z)
-    columns = (
-        [(from_prev_x, 0, 96, 8, il * 4, il) for il in range(2)],
-        [(None, 0, 0, 48, (x + 2) * 4, x) for x in range(8)],
-        [(from_next_x, 0, 96, 8, il * 4, 6 + il) for il in range(2)],
-    )
-    for column, entries in enumerate(columns):
-        for by in range(4):
-            totals = [None, None]
-            for ref, base_o, base_z, step, start, x in entries:
-                upper = field[pl.ds(40 * x + 8 * by, 8), :]
-                lower = field[pl.ds(40 * x + 8 * by + 8, 4), :]
-                for half in range(2):
-                    w = ref if ref is not None else (wo, wz)[half]
-                    first = (base_o, base_z)[half] + start + by
-                    w8 = w[pl.ds(first, 8, stride=step), :]
-                    w4 = w[pl.ds(first + 8 * step, 4, stride=step), :]
-                    terms = (w8 * upper, w4 * lower)
-                    if totals[half] is None:
-                        totals[half] = terms
-                    else:
-                        totals[half] = tuple(a + b for a, b in zip(totals[half], terms))
-            for half, sums in enumerate((sums_o, sums_z)):
-                a8, a4 = totals[half]
-                line = jnp.sum(a8, axis=0, keepdims=True) + jnp.sum(a4, axis=0, keepdims=True)
-                sums[pl.ds((by + 1) * 8 + column, 1), :] = line
+    for by in range(4):
+        totals = [None, None]
+        for i in range(12):
+            upper = field[pl.ds(40 * i + 8 * by, 8), :]
+            lower = field[pl.ds(40 * i + 8 * by + 8, 4), :]
+            for half, w in enumerate((wo, wz)):
+                terms = (
+                    w[pl.ds(4 * i + by, 8, stride=48), :] * upper,
+                    w[pl.ds(4 * i + by + 384, 4, stride=48), :] * lower,
+                )
+                old = totals[half]
+                totals[half] = terms if old is None else (old[0] + terms[0], old[1] + terms[1])
+        for half, sums in enumerate((sums_o, sums_z)):
+            a8, a4 = totals[half]
+            sums[pl.ds(by + 1, 1), :] = jnp.sum(a8, axis=0, keepdims=True) + jnp.sum(a4, axis=0, keepdims=True)
     for side, (by, first_row, strip) in enumerate(((-1, 2, from_prev_y), (4, 32, from_next_y))):
         for half, sums in enumerate((sums_o, sums_z)):
             total = None
             for n in range(2):
-                tile = strip[pl.ds((2 * n + half) * 12 + 2, 8), :]
+                tile = strip[pl.ds((2 * n + half) * 12, 12), :]
                 if half:
-                    tile = faced(core, tile, facing_y[pl.ds(side * 24 + n * 12 + 2, 8), :])
-                line = tile * field[pl.ds(first_row + n, 8, stride=40), :]
+                    tile = faced(core, tile, facing_y[pl.ds(side * 24 + n * 12, 12), :])
+                line = tile * field[pl.ds(first_row + n, 12, stride=40), :]
                 total = line if total is None else total + line
-            sums[pl.ds((by + 1) * 8 + 1, 1), :] = jnp.sum(total, axis=0, keepdims=True)
-
-
-def tail_kernel(field, sums_o, sums_z, corners, facing_x, message, whole, done_o, done_z, pattern):
-    core = lax.axis_index("gz")
-    at = iota((32, 128), 0)
-    whole[...] = jnp.where((at % 8) // 2 % 2 == 1, faced(core, corners[...], facing_x[...]), corners[...])
-    done_o[...] = sums_o[...]
-    done_z[...] = sums_z[...]
-    for side, (by, first_row) in enumerate(((-1, 2), (4, 32))):
-        for half, sums in enumerate((done_o, done_z)):
-            for column, first_x in ((0, 0), (2, 6)):
-                total = None
-                for n in range(2):
-                    tile = whole[pl.ds(column * 8 + side * 8 + (2 * n + half) * 2, 2), :]
-                    line = tile * field[pl.ds(40 * first_x + first_row + n, 2, stride=40), :]
-                    total = line if total is None else total + line
-                sums[pl.ds((by + 1) * 8 + column, 1), :] = jnp.sum(total, axis=0, keepdims=True)
+            sums[pl.ds(by + 1, 1), :] = jnp.sum(total, axis=0, keepdims=True)
     inside, reach = spread(core)
-    out = dot3(done_o[...], inside) + dot3(done_z[...], reach)
-    level = [out[8 * n : 8 * n + 8] for n in range(6)]
-    group = iota((8, 128), 1) // 32
-    group1 = iota((1, 128), 1) // 32
+    out = dot3(sums_o[...], inside) + dot3(sums_z[...], reach)
+    group = iota((1, 128), 1) // 32
+    lines = [out[n : n + 1] for n in range(6)]
+    row = iota((8, 128), 0)
+    mask = (iota((8, 128), 1) == 64 + row) & (row < 6)
+    across = jnp.sum(jnp.where(mask, out, 0.0), axis=0, keepdims=True)
     halves = []
     for zc in range(2):
-        total = jnp.zeros((8, 128), F32)
+        total = jnp.zeros((1, 128), F32)
+        ends = across
         for by in range(4):
             shift = (by * 32 - zc * 32) % 128
-            moved = pltpu.roll(level[by + 1], shift, 1) if shift else level[by + 1]
-            total = jnp.where(group == by, moved, total)
-        hooks = [[], []]
-        for n in range(4):
+            total = jnp.where(group == by, pltpu.roll(lines[by + 1], shift, 1) if shift else lines[by + 1], total)
+        for n, line in ((0, lines[5]), (1, lines[0])):
             shift = (n * 32 - zc * 32) % 128
-            value = level[5] if n % 2 == 0 else level[0]
-            value = pltpu.roll(value, shift, 1) if shift else value
-            hooks[0].append(value[n // 2 : n // 2 + 1])
-            hooks[1].append(value[2:3])
-        fourth = jnp.where(
-            group1 == 0, hooks[0][0], jnp.where(group1 == 1, hooks[0][1], jnp.where(group1 == 2, hooks[0][2], hooks[0][3]))
-        )
-        fifth = jnp.where(group1 == 0, hooks[1][0], hooks[1][1])
-        halves.append((total[0:3], fourth, fifth))
+            ends = jnp.where(group == n, pltpu.roll(line, shift, 1) if shift else line, ends)
+        halves.append((total, ends))
     first = core == 0
-    row = iota((48, 128), 0)
-    mask = (iota((48, 128), 1) == 64 + (row // 8) * 4 + row % 8) & (row % 8 < 3)
-    across = jnp.sum(jnp.where(mask, out, 0.0), axis=0, keepdims=True)
-    for n in range(8):
-        pattern[pl.ds(5 * n, 3), :] = jnp.where(first, halves[0][0], halves[1][0])
-        pattern[pl.ds(5 * n + 3, 1), :] = jnp.where(first, halves[0][1], halves[1][1])
-        pattern[pl.ds(5 * n + 4, 1), :] = jnp.where(
-            group1 < 2, jnp.where(first, halves[0][2], halves[1][2]), across
-        )
-    block = pattern[...]
-    for n in range(message.shape[0] // 40):
-        message[pl.ds(40 * n, 40), :] = block
+    own = jnp.where(first, halves[0][0], halves[1][0])
+    ends = jnp.where(first, halves[0][1], halves[1][1])
+    block = jnp.where(row % 2 == 0, own, ends)
+    for n in range(message.shape[0] // 8):
+        message[pl.ds(8 * n, 8), :] = block
 
 
 def gather_kernel(shared, own, padded):
@@ -350,37 +328,30 @@
     size_x = lax.axis_size("gx")
     padded[...] = jnp.zeros_like(padded)
     for x in range(size_x):
-        padded[pl.ds((x + 5) * 60 + 10, 40), :] = shared[pl.ds(x * 40, 40), :]
+        padded[pl.ds((x + 4) * 24 + 4, 16), :] = shared[pl.ds(x * 16, 16), :]
     lane = iota((9, 128), 1)
     source = iota((128, 128), 0)
     target = iota((128, 128), 1)
-    edge = 31 * core
     at = target // 32
-    hit = target % 32 == edge
+    hit = target % 32 == 31 * core
 
     def place(mask):
         return jnp.where(mask, 1.0, 0.0).astype(BF16)
 
-    within = place(hit & (source == 68 + 4 * at))
-    lower = place(hit & (at == 0) & (source == 84))
+    within = place(hit & (source == 65 + at))
+    lower = place(hit & (at == 0) & (source == 69))
     upper = place(hit & (at == 3) & (source == 64))
 
-    def line(dx, dy, kind):
-        return padded[pl.ds(((gx + 1 + dx) * 12 + gy + 2 + dy) * 5 + kind, 9, stride=60), :]
-
-    beyond, before, across = [], [], []
-    for dy in range(-2, 3):
-        a, b, c, d, e = line(1, dy, 3), line(0, dy, 3), line(-1, dy, 4), line(1, dy, 4), line(0, dy, 4)
-        beyond.append(a + pltpu.roll(b, 64, 1) + c)
-        before.append(pltpu.roll(a, 64, 1) + b + pltpu.roll(c, 64, 1))
-        across.append(d + pltpu.roll(e, 127, 1) + pltpu.roll(c, 126, 1))
+    def line(dy, kind):
+        return padded[pl.ds((gx * 12 + gy + 2 + dy) * 2 + kind, 9, stride=24), :]
+
+    ends = [line(dy, 1) for dy in range(-2, 3)]
     own[...] = jnp.zeros_like(own)
     for yc in range(3):
-        total = line(1, yc - 1, 0) + line(0, yc - 1, 1) + line(-1, yc - 1, 2)
-        total = total + jnp.where(lane < 32, beyond[yc], jnp.where(lane >= 96, before[yc + 2], 0.0))
-        own[pl.ds(16 * yc, 9), :] = total
+        extra = jnp.where(lane >= 96, pltpu.roll(ends[yc + 2], 64, 1), 0.0)
+        own[pl.ds(16 * yc, 9), :] = line(yc - 1, 0) + jnp.where(lane < 32, ends[yc], extra)
         own[pl.ds(48 + 16 * yc, 9), :] = (
-            dot3(across[yc + 1], within) + dot3(across[yc], lower) + dot3(across[yc + 2], upper)
+            dot3(ends[yc + 1], within) + dot3(ends[yc], lower) + dot3(ends[yc + 2], upper)
         )
 
 
@@ -390,8 +361,8 @@
 
 
 def solve_kernel(
-    own, other, coefs, wo, wz, from_prev_x, from_next_x, from_prev_y, from_next_y, facing_y, corners, pressure,
-    solution, new_pressure, start, state, blocks, field,
+    own, other, coefs, wo, wz, from_prev_x, from_next_x, from_prev_y, from_next_y, facing_y, tips, facing_x, pressure,
+    solution, new_pressure, start, state, blocks, field, corners,
 ):
     gx = lax.axis_index("gx")
     gy = lax.axis_index("gy")
@@ -399,6 +370,8 @@
     size_x = lax.axis_size("gx")
     size_y = lax.axis_size("gy")
 
+    tip = iota((32, 128), 0)
+    corners[...] = jnp.where((tip % 8) // 2 % 2 == 1, faced(core, tips[...], facing_x[...]), tips[...])
     at_x = iota((9, 128), 0) + gx - 4
     valid_x = (at_x >= 0) & (at_x < size_x)
     for yc in range(3):
@@ -578,39 +551,39 @@
     facing = shift(wz, "gz", 1)
     facing_p = shift(pressure, "gz", 1)
     facing_t = shift(trans_z, "gz", 1)
-    wz, to_next_x, to_prev_x, strips = call(
-        relay_kernel, [shape(576, 128), shape(368, 128), shape(336, 128), shape(48, 128)]
-    )(wo, wz, facing, pressure, trans_x, coarse, from_prev_y, from_next_y)
-    from_prev_x = shift(to_next_x, "gx", 1)
-    from_next_x = shift(to_prev_x, "gx", -1)
-    facing_y = shift(strips, "gz", 1)
-
-    corners, up, down = call(collect_kernel, [shape(32, 128), shape(224, 128, dtype=BF16), shape(224, 128, dtype=BF16)])(
-        from_prev_x, from_next_x, to_next_x
-    )
-    facing_x = shift(corners, "gz", 1)
     wells = call(wells_kernel, shape(256, 128))(well_cells.reshape(8, 128), well_rates.reshape(8, 128))
     partial = call(local_kernel, shape(8, 32, 128))(
         pressure, accumulation, trans_x, trans_y, trans_z, source, wells, facing_p, facing_t, from_prev_y, from_next_y
     )
-    residual, field, sums_o, sums_z = call(
-        sums_kernel, [shape(8, 32, 128), shape(320, 128), shape(48, 128), shape(48, 128)]
-    )(partial, pressure, trans_x, wo, wz, from_prev_x, from_next_x, from_prev_y, from_next_y, facing_y)
+    wz, near_next, near_prev, to_next_x, to_prev_x, strips = call(
+        relay_kernel,
+        [shape(576, 128), shape(128, 128), shape(96, 128), shape(304, 128), shape(304, 128), shape(48, 128)],
+    )(wo, wz, facing, partial, pressure, trans_x, coarse, from_prev_y, from_next_y)
+    near_from_prev = shift(near_next, "gx", 1)
+    near_from_next = shift(near_prev, "gx", -1)
+    facing_y = shift(strips, "gz", 1)
+    from_prev_x = shift(to_next_x, "gx", 1)
+    from_next_x = shift(to_prev_x, "gx", -1)
+
     count = lax.axis_size("gx") * lax.axis_size("gy")
-    message, corners = call(
-        tail_kernel,
-        [shape(5 * count, 128), shape(32, 128)],
-        [pltpu.VMEM((48, 128), F32), pltpu.VMEM((48, 128), F32), pltpu.VMEM((40, 128), F32)],
-    )(field, sums_o, sums_z, corners, facing_x)
-    shared = lax.all_to_all(message.reshape(count, 1, 640), ("gx", "gy"), 0, 0)
-    shared = shared.reshape(5 * count, 128)
-
+    residual, message = call(
+        sums_kernel,
+        [shape(8, 32, 128), shape(2 * count, 128)],
+        [pltpu.VMEM((480, 128), F32), pltpu.VMEM((8, 128), F32), pltpu.VMEM((8, 128), F32)],
+    )(partial, pressure, trans_x, wo, wz, near_from_prev, near_from_next, from_prev_y, from_next_y, facing_y)
+    shared = lax.all_to_all(message.reshape(count, 1, 256), ("gx", "gy"), 0, 0)
+    shared = shared.reshape(2 * count, 128)
+
+    tips, up, down = call(
+        collect_kernel, [shape(32, 128), shape(224, 128, dtype=BF16), shape(224, 128, dtype=BF16)]
+    )(from_prev_x, from_next_x, to_next_x)
+    facing_x = shift(tips, "gz", 1)
     near = call(window_kernel, shape(688, 128))(
         shift(up, "gx", 3), shift(down, "gx", -3), from_prev_x, to_next_x, from_next_x
     )
     coefs = call(stack_kernel, shape(1376, 128))(near, shift(near, "gz", 1))
 
-    own = call(gather_kernel, shape(96, 128), [pltpu.VMEM((26 * 60, 128), F32)])(shared)
+    own = call(gather_kernel, shape(96, 128), [pltpu.VMEM((576, 128), F32)])(shared)
     other = shift(own, "gz", 1)
     solution, new_pressure = call(
         solve_kernel,
@@ -620,8 +593,9 @@
             pltpu.VMEM((96, 128), F32),
             pltpu.VMEM((48, 128), F32),
             pltpu.VMEM((320, 128), F32),
+            pltpu.VMEM((32, 128), F32),
         ],
-    )(own, other, coefs, wo, wz, from_prev_x, from_next_x, from_prev_y, from_next_y, facing_y, corners, pressure)
+    )(own, other, coefs, wo, wz, from_prev_x, from_next_x, from_prev_y, from_next_y, facing_y, tips, facing_x, pressure)
     return residual, solution, new_pressure
 
 

time: 66.3 us -> 71.9 us (1.084)
  blocking collectives: 0 us -> 19.3 us
  starting transfers between devices: 45.7 us -> 36.2 us
  waiting for transfers between devices: 11.8 us -> 8.78 us
  Pallas kernels: 7.74 us -> 6.56 us
    all_to_all x0 -> x1, blocking collectives: none -> 19.3 us  [on_device(): shared = lax.all_to_all(message.reshape(count, 1, 256), ('gx', 'gy'), 0, 0)]
    all_to_all x1 -> x0, starting transfers between devices: 12.4 us -> none  [on_device(): shared = lax.all_to_all(message.reshape(count, 1, 640), ('gx', 'gy'), 0, 0)]
    ppermute x13 -> x15, waiting for transfers between devices: 11.8 us -> 8.78 us  [shift(): lax.ppermute(value, axis, [(i, (i + steps) % count) for i in range(count)])]
    ppermute x13 -> x15, starting transfers between devices: 33.3 us -> 36.2 us  [shift(): lax.ppermute(value, axis, [(i, (i + steps) % count) for i in range(count)])]
    pallas_call x4 -> x3, Pallas kernels: 2.55 us -> 1.29 us  [the longest x1 0.82 us: on_device(): call(sums_kernel, [shape(8, 32, 128), shape(2 * count, 128)], [pltpu.VMEM...]
  transfers between devices with their start and end apart: 14 -> 15, of which waited for: 4 -> 4; matrix products, arithmetic and copies ran while one was open for 0% -> 0% of each run, Pallas kernels for 3% -> 3%
where the time goes in v1:
time: 71.9 us; the launch traced here: 71.7 us
  starting transfers between devices  36.2 us (50%)
  blocking collectives  19.3 us (27%)
  waiting for transfers between devices  8.78 us (12%)
  Pallas kernels  6.56 us (9%)
  between operations  0.8 us (1%)
    ppermute x15, starting transfers between devices, shift(): lax.ppermute(value, axis, [(i, (i + steps) % count) for i in range(count)])  36.2 us
    all_to_all x1, blocking collectives, on_device(): shared = lax.all_to_all(message.reshape(count, 1, 256), ('gx', 'gy'), 0, 0)  19.3 us
    ppermute x15, waiting for transfers between devices, shift(): lax.ppermute(value, axis, [(i, (i + steps) % count) for i in range(count)])  8.78 us
    pallas_call x1, Pallas kernels, on_device(): call(solve_kernel, [shape(1, 4, 32), shape(8, 32, 128)], [pltpu.VMEM((96,...  2.43 us
    pallas_call x1, Pallas kernels, on_device(): call(pack_kernel, [shape(576, 128), shape(576, 128), shape(96, 128), shap...  1.88 us
  transfers between devices with their start and end apart: 15, of which 4 were waited for; matrix products, arithmetic and copies ran while one was open for 0% of the time, Pallas kernels for 3%

profile of v1, /device:TPU:1, one launch (start us, length us, event | category | flops | bytes accessed | tf_op | source)
XLA Modules:
  0.0 71.7 jit_solution(3595783071163748003)
XLA Ops:
  0.6 0.0 copy-start
  0.6 0.0 copy-start.4
  0.7 0.0 copy-start.6
  0.7 0.0 copy-start.7
  0.7 0.0 copy-start.2
  0.7 0.0 copy-start.3
  0.7 0.0 copy-start.5
  0.7 1.9 %shard_map.131 = (f32[576,128]{1,0:T(8,128)S(1)}, f32[576,128]{1,0:T(8,128)S(1)}, f32[96,128]{1,0:T(8,128)S(1)}, f32[88,128]{1,0:T(8,128)S(1)}, f32[32,128]{1,0:T(8,128)S(1)}) custom-call(bf16[6,576,32]{2,1,0:T(8,128)(2,1)} %bitcast.9, f32[8,32,128]{2,1,0:T(8,128)} %pressure.7, f32[8,32,128]{2,1,0:T(8,128)} %trans_y.1, f32[26,1,4,32]{3,2,1,0:T(4,128)} %coarse_off_in.1, ...), custom_call_target="tpu_custom_call" | custom-call | tf_op jit(solution)/shard_map/pallas_call | solution.py:531
  2.6 0.0 copy-start.1
  2.6 3.3 %collective-permute-start.4 = (f32[576,128]{1,0:T(8,128)S(1)}, f32[576,128]{1,0:T(8,128)S(1)}, u32[]{:S(2)}, u32[]{:S(2)}) collective-permute-start(f32[576,128]{1,0:T(8,128)S(1)} %get-tuple-element.24.wz), channel_id=1, source_target_pairs={{0,1},{1,0},{2,3},{3,2},{4,5},{5,4},{6,7},{7,6},{8,9},{9,8},{10,11... | collective-permute-start | bytes 884744 | tf_op jit(solution)/shard_map/ppermute | solution.py:525
  5.9 0.0 copy-done
  5.9 0.1 collective-permute-start
  6.0 0.4 collective-permute-start.1
  6.4 5.2 %collective-permute-start.2 = (f32[96,128]{1,0:T(8,128)S(1)}, f32[96,128]{1,0:T(8,128)S(1)}, u32[]{:S(2)}, u32[]{:S(2)}) collective-permute-start(f32[96,128]{1,0:T(8,128)S(1)} %get-tuple-element.21), channel_id=1, source_target_pairs={{0,2},{2,4},{4,6},{6,8},{8,10},{10,12},{12,14},{14,0},{1,3},{3,5},... | collective-permute-start | bytes 147464 | tf_op jit(solution)/shard_map/ppermute | solution.py:525
  11.6 2.4 %collective-permute-start.3 = (f32[88,128]{1,0:T(8,128)S(1)}, f32[88,128]{1,0:T(8,128)S(1)}, u32[]{:S(2)}, u32[]{:S(2)}) collective-permute-start(f32[88,128]{1,0:T(8,128)S(1)} %get-tuple-element.22), channel_id=1, source_target_pairs={{0,14},{2,0},{4,2},{6,4},{8,6},{10,8},{12,10},{14,12},{1,15},{3,1}... | collective-permute-start | bytes 135176 | tf_op jit(solution)/shard_map/ppermute | solution.py:525
  14.1 0.6 shard_map.130.wells
  14.7 3.9 %collective-permute-done.3.from_next_y = f32[88,128]{1,0:T(8,128)S(1)} collective-permute-done((f32[88,128]{1,0:T(8,128)S(1)}, f32[88,128]{1,0:T(8,128)S(1)}, u32[]{:S(2)}, u32[]{:S(2)}) %collective-permute-start.3) | collective-permute-done | bytes 45088 | tf_op jit(solution)/shard_map/ppermute | solution.py:525
  18.5 0.0 collective-permute-done.2.from_prev_y
  18.5 0.0 collective-permute-done.facing_p
  18.5 0.0 collective-permute-done.1.facing_t
  18.6 0.3 shard_map.132.partial
  18.9 0.0 collective-permute-done.4.facing
  18.9 0.2 shard_map.133
  19.0 1.3 %collective-permute-start.9 = (f32[304,128]{1,0:T(8,128)S(1)}, f32[304,128]{1,0:T(8,128)S(1)}, u32[]{:S(2)}, u32[]{:S(2)}) collective-permute-start(f32[304,128]{1,0:T(8,128)S(1)} %get-tuple-element.32.own), channel_id=1, source_target_pairs={{0,16},{16,32},{32,48},{48,64},{64,80},{80,96},{96,112},{112,128},... | collective-permute-start | bytes 466952 | tf_op jit(solution)/shard_map/ppermute | solution.py:525
  20.3 4.2 %collective-permute-start.10 = (f32[304,128]{1,0:T(8,128)S(1)}, f32[304,128]{1,0:T(8,128)S(1)}, u32[]{:S(2)}, u32[]{:S(2)}) collective-permute-start(f32[304,128]{1,0:T(8,128)S(1)} %get-tuple-element.33), channel_id=1, source_target_pairs={{0,240},{16,0},{32,16},{48,32},{64,48},{80,64},{96,80},{112,96},{1... | collective-permute-start | bytes 466952 | tf_op jit(solution)/shard_map/ppermute | solution.py:525
  24.5 2.6 %collective-permute-done.9.from_prev_x = f32[304,128]{1,0:T(8,128)S(1)} collective-permute-done((f32[304,128]{1,0:T(8,128)S(1)}, f32[304,128]{1,0:T(8,128)S(1)}, u32[]{:S(2)}, u32[]{:S(2)}) %collective-permute-start.9) | collective-permute-done | bytes 155680 | tf_op jit(solution)/shard_map/ppermute | solution.py:525
  27.1 0.0 collective-permute-done.10.from_next_x
  27.1 1.4 %collective-permute-start.11 = (bf16[224,128]{1,0:T(8,128)(2,1)S(1)}, bf16[224,128]{1,0:T(8,128)(2,1)S(1)}, u32[]{:S(2)}, u32[]{:S(2)}) collective-permute-start(bf16[224,128]{1,0:T(8,128)(2,1)S(1)} %get-tuple-element.34), channel_id=1, source_target_pairs={{0,48},{16,64},{32,80},{48,96},{64,112},{80,128},{96,144},{112,160... | collective-permute-start | bytes 172040 | tf_op jit(solution)/shard_map/ppermute | solution.py:525
  28.5 2.8 %collective-permute-start.12 = (bf16[224,128]{1,0:T(8,128)(2,1)S(1)}, bf16[224,128]{1,0:T(8,128)(2,1)S(1)}, u32[]{:S(2)}, u32[]{:S(2)}) collective-permute-start(bf16[224,128]{1,0:T(8,128)(2,1)S(1)} %get-tuple-element.35), channel_id=1, source_target_pairs={{0,208},{16,224},{32,240},{48,0},{64,16},{80,32},{96,48},{112,64},... | collective-permute-start | bytes 172040 | tf_op jit(solution)/shard_map/ppermute | solution.py:525
  31.4 0.0 collective-permute-start.5
  31.4 5.4 %collective-permute-start.6 = (f32[96,128]{1,0:T(8,128)S(1)}, f32[96,128]{1,0:T(8,128)S(1)}, u32[]{:S(2)}, u32[]{:S(2)}) collective-permute-start(f32[96,128]{1,0:T(8,128)S(1)} %get-tuple-element.28), channel_id=1, source_target_pairs={{0,240},{16,0},{32,16},{48,32},{64,48},{80,64},{96,80},{112,96},{1... | collective-permute-start | bytes 147464 | tf_op jit(solution)/shard_map/ppermute | solution.py:525
  36.7 0.0 collective-permute-done.11.up
  36.7 0.0 collective-permute-done.12.down
  36.8 3.8 %collective-permute-start.13 = (f32[688,128]{1,0:T(8,128)S(1)}, f32[688,128]{1,0:T(8,128)S(1)}, u32[]{:S(2)}, u32[]{:S(2)}) collective-permute-start(f32[688,128]{1,0:T(8,128)S(1)} %shard_map.137.near), channel_id=1, source_target_pairs={{0,1},{1,0},{2,3},{3,2},{4,5},{5,4},{6,7},{7,6},{8,9},{9,8},{10,11... | collective-permute-start | bytes 1056776 | tf_op jit(solution)/shard_map/ppermute | solution.py:525
  40.6 0.1 collective-permute-start.7
  40.7 1.2 %collective-permute-done.7.facing_y = f32[48,128]{1,0:T(8,128)S(1)} collective-permute-done((f32[48,128]{1,0:T(8,128)S(1)}, f32[48,128]{1,0:T(8,128)S(1)}, u32[]{:S(2)}, u32[]{:S(2)}) %collective-permute-start.7) | collective-permute-done | bytes 24608 | tf_op jit(solution)/shard_map/ppermute | solution.py:525
  41.9 0.0 collective-permute-done.6.near_from_next
  41.9 0.0 collective-permute-done.5.near_from_prev
  41.9 0.8 %shard_map.134 = (f32[8,32,128]{2,1,0:T(8,128)}, f32[256,128]{1,0:T(8,128)S(1)}) custom-call(f32[8,32,128]{2,1,0:T(8,128)S(1)} %shard_map.132.partial, f32[8,32,128]{2,1,0:T(8,128)S(1)} %copy-done, f32[8,32,128]{2,1,0:T(8,128)S(1)} %copy-done.1, f32[576,128]{1,0:T(8,128)S(1)} %get-tuple-element.23.wo, f32[576,128]{1,0:T(8,128)S(1)} %get-tuple-element.26.wz, ...), custom_call_target="tpu_custom_call" | custom-call | tf_op jit(solution)/shard_map/pallas_call | solution.py:569
  42.7 19.3 %all_to_all.5 = f32[128,1,256]{2,1,0:T(1,128)S(1)} all-to-all(f32[128,1,256]{2,1,0:T(1,128)S(1)} %bitcast.6), channel_id=1, replica_groups=mesh['gx'=16,'gy'=8,'gz'=2] {'gx','gy'}, dimensions={0} | all-to-all | bytes 262144 | tf_op jit(solution)/shard_map/all_to_all | solution.py:574
  62.1 0.3 shard_map.135.own
  62.4 5.7 %collective-permute-start.8 = (f32[96,128]{1,0:T(8,128)S(1)}, f32[96,128]{1,0:T(8,128)S(1)}, u32[]{:S(2)}, u32[]{:S(2)}) collective-permute-start(f32[96,128]{1,0:T(8,128)S(1)} %shard_map.135.own), channel_id=1, source_target_pairs={{0,1},{1,0},{2,3},{3,2},{4,5},{5,4},{6,7},{7,6},{8,9},{9,8},{10,11... | collective-permute-start | bytes 147464 | tf_op jit(solution)/shard_map/ppermute | solution.py:525
  68.1 0.1 collective-permute-start.14
  68.2 0.0 collective-permute-done.13.far
  68.2 0.1 shard_map.138.coefs
  68.2 1.0 %collective-permute-done.14.facing_x = f32[32,128]{1,0:T(8,128)S(1)} collective-permute-done((f32[32,128]{1,0:T(8,128)S(1)}, f32[32,128]{1,0:T(8,128)S(1)}, u32[]{:S(2)}, u32[]{:S(2)}) %collective-permute-start.14) | collective-permute-done | bytes 16416 | tf_op jit(solution)/shard_map/ppermute | solution.py:525
  69.3 0.0 collective-permute-done.8.other
  69.3 2.4 %shard_map.139 = (f32[1,4,32]{2,1,0:T(4,128)}, f32[8,32,128]{2,1,0:T(8,128)}) custom-call(f32[96,128]{1,0:T(8,128)S(1)} %shard_map.135.own, f32[96,128]{1,0:T(8,128)S(1)} %collective-permute-done.8.other, f32[1376,128]{1,0:T(8,128)S(1)} %shard_map.138.coefs, f32[576,128]{1,0:T(8,128)S(1)} %get-tuple-element.23.wo, f32[576,128]{1,0:T(8,128)S(1)} %get-tuple-element.26.wz, ...), custom_call_target="tpu_custom_call" | custom-call | tf_op jit(solution)/shard_map/pallas_call | solution.py:588
  (9 shorter events, 0.1 us)
Async XLA Ops:
  0.6 5.3 %copy-start = (f32[8,32,128]{2,1,0:T(8,128)S(1)}, f32[8,32,128]{2,1,0:T(8,128)}, u32[]{:S(2)}) copy-start(f32[8,32,128]{2,1,0:T(8,128)} %pressure.7) | copy-start | bytes 393220
  0.6 5.4 %copy-start.4 = (f32[8,32,128]{2,1,0:T(8,128)S(1)}, f32[8,32,128]{2,1,0:T(8,128)}, u32[]{:S(2)}) copy-start(f32[8,32,128]{2,1,0:T(8,128)} %trans_z.1) | copy-start | bytes 393220
  0.7 13.4 %copy-start.6 = (s32[1024]{0:T(1024)S(1)}, s32[1024]{0:T(1024)}, u32[]{:S(2)}) copy-start(s32[1024]{0:T(1024)} %param.17) | copy-start | bytes 12292
  0.7 13.4 %copy-start.7 = (f32[1024]{0:T(1024)S(1)}, f32[1024]{0:T(1024)}, u32[]{:S(2)}) copy-start(f32[1024]{0:T(1024)} %param.18) | copy-start | bytes 12292
  0.7 17.9 %copy-start.2 = (f32[8,32,128]{2,1,0:T(8,128)S(1)}, f32[8,32,128]{2,1,0:T(8,128)}, u32[]{:S(2)}) copy-start(f32[8,32,128]{2,1,0:T(8,128)} %trans_y.1) | copy-start | bytes 393220
  0.7 17.9 %copy-start.3 = (f32[8,32,128]{2,1,0:T(8,128)S(1)}, f32[8,32,128]{2,1,0:T(8,128)}, u32[]{:S(2)}) copy-start(f32[8,32,128]{2,1,0:T(8,128)} %accumulation.1) | copy-start | bytes 393220
  0.7 17.9 %copy-start.5 = (f32[8,32,128]{2,1,0:T(8,128)S(1)}, f32[8,32,128]{2,1,0:T(8,128)}, u32[]{:S(2)}) copy-start(f32[8,32,128]{2,1,0:T(8,128)} %source.1) | copy-start | bytes 393220
  2.6 16.0 %copy-start.1 = (f32[8,32,128]{2,1,0:T(8,128)S(1)}, f32[8,32,128]{2,1,0:T(8,128)}, u32[]{:S(2)}) copy-start(f32[8,32,128]{2,1,0:T(8,128)} %trans_x.5) | copy-start | bytes 393220
  2.6 16.3 %collective-permute-start.4 = (f32[576,128]{1,0:T(8,128)S(1)}, f32[576,128]{1,0:T(8,128)S(1)}, u32[]{:S(2)}, u32[]{:S(2)}) collective-permute-start(f32[576,128]{1,0:T(8,128)S(1)} %get-tuple-element.24.wz), channel_id=1, source_target_pairs={{0,1},{1,0},{2,3},{3,2},{4,5},{5,4},{6,7},{7,6},{8,9},{9,8},{10,11... | collective-permute-start | bytes 884744 | tf_op jit(solution)/shard_map/ppermute | solution.py:525
  5.9 12.6 %collective-permute-start = (f32[8,32,128]{2,1,0:T(8,128)S(1)}, f32[8,32,128]{2,1,0:T(8,128)S(1)}, u32[]{:S(2)}, u32[]{:S(2)}) collective-permute-start(f32[8,32,128]{2,1,0:T(8,128)S(1)} %copy-done), channel_id=1, source_target_pairs={{0,1},{1,0},{2,3},{3,2},{4,5},{5,4},{6,7},{7,6},{8,9},{9,8},{10,11... | collective-permute-start | bytes 393224 | tf_op jit(solution)/shard_map/ppermute | solution.py:525
  6.0 12.5 %collective-permute-start.1 = (f32[8,32,128]{2,1,0:T(8,128)S(1)}, f32[8,32,128]{2,1,0:T(8,128)S(1)}, u32[]{:S(2)}, u32[]{:S(2)}) collective-permute-start(f32[8,32,128]{2,1,0:T(8,128)S(1)} %copy-done.4), channel_id=1, source_target_pairs={{0,1},{1,0},{2,3},{3,2},{4,5},{5,4},{6,7},{7,6},{8,9},{9,8},{10,11... | collective-permute-start | bytes 393224 | tf_op jit(solution)/shard_map/ppermute | solution.py:525
  6.4 12.1 %collective-permute-start.2 = (f32[96,128]{1,0:T(8,128)S(1)}, f32[96,128]{1,0:T(8,128)S(1)}, u32[]{:S(2)}, u32[]{:S(2)}) collective-permute-start(f32[96,128]{1,0:T(8,128)S(1)} %get-tuple-element.21), channel_id=1, source_target_pairs={{0,2},{2,4},{4,6},{6,8},{8,10},{10,12},{12,14},{14,0},{1,3},{3,5},... | collective-permute-start | bytes 147464 | tf_op jit(solution)/shard_map/ppermute | solution.py:525
  11.6 6.9 %collective-permute-start.3 = (f32[88,128]{1,0:T(8,128)S(1)}, f32[88,128]{1,0:T(8,128)S(1)}, u32[]{:S(2)}, u32[]{:S(2)}) collective-permute-start(f32[88,128]{1,0:T(8,128)S(1)} %get-tuple-element.22), channel_id=1, source_target_pairs={{0,14},{2,0},{4,2},{6,4},{8,6},{10,8},{12,10},{14,12},{1,15},{3,1}... | collective-permute-start | bytes 135176 | tf_op jit(solution)/shard_map/ppermute | solution.py:525
  19.0 8.1 %collective-permute-start.9 = (f32[304,128]{1,0:T(8,128)S(1)}, f32[304,128]{1,0:T(8,128)S(1)}, u32[]{:S(2)}, u32[]{:S(2)}) collective-permute-start(f32[304,128]{1,0:T(8,128)S(1)} %get-tuple-element.32.own), channel_id=1, source_target_pairs={{0,16},{16,32},{32,48},{48,64},{64,80},{80,96},{96,112},{112,128},... | collective-permute-start | bytes 466952 | tf_op jit(solution)/shard_map/ppermute | solution.py:525
  20.3 6.8 %collective-permute-start.10 = (f32[304,128]{1,0:T(8,128)S(1)}, f32[304,128]{1,0:T(8,128)S(1)}, u32[]{:S(2)}, u32[]{:S(2)}) collective-permute-start(f32[304,128]{1,0:T(8,128)S(1)} %get-tuple-element.33), channel_id=1, source_target_pairs={{0,240},{16,0},{32,16},{48,32},{64,48},{80,64},{96,80},{112,96},{1... | collective-permute-start | bytes 466952 | tf_op jit(solution)/shard_map/ppermute | solution.py:525
  27.1 9.6 %collective-permute-start.11 = (bf16[224,128]{1,0:T(8,128)(2,1)S(1)}, bf16[224,128]{1,0:T(8,128)(2,1)S(1)}, u32[]{:S(2)}, u32[]{:S(2)}) collective-permute-start(bf16[224,128]{1,0:T(8,128)(2,1)S(1)} %get-tuple-element.34), channel_id=1, source_target_pairs={{0,48},{16,64},{32,80},{48,96},{64,112},{80,128},{96,144},{112,160... | collective-permute-start | bytes 172040 | tf_op jit(solution)/shard_map/ppermute | solution.py:525
  28.5 8.2 %collective-permute-start.12 = (bf16[224,128]{1,0:T(8,128)(2,1)S(1)}, bf16[224,128]{1,0:T(8,128)(2,1)S(1)}, u32[]{:S(2)}, u32[]{:S(2)}) collective-permute-start(bf16[224,128]{1,0:T(8,128)(2,1)S(1)} %get-tuple-element.35), channel_id=1, source_target_pairs={{0,208},{16,224},{32,240},{48,0},{64,16},{80,32},{96,48},{112,64},... | collective-permute-start | bytes 172040 | tf_op jit(solution)/shard_map/ppermute | solution.py:525
  31.4 10.5 %collective-permute-start.5 = (f32[128,128]{1,0:T(8,128)S(1)}, f32[128,128]{1,0:T(8,128)S(1)}, u32[]{:S(2)}, u32[]{:S(2)}) collective-permute-start(f32[128,128]{1,0:T(8,128)S(1)} %get-tuple-element.27), channel_id=1, source_target_pairs={{0,16},{16,32},{32,48},{48,64},{64,80},{80,96},{96,112},{112,128},... | collective-permute-start | bytes 196616 | tf_op jit(solution)/shard_map/ppermute | solution.py:525
  31.4 10.5 %collective-permute-start.6 = (f32[96,128]{1,0:T(8,128)S(1)}, f32[96,128]{1,0:T(8,128)S(1)}, u32[]{:S(2)}, u32[]{:S(2)}) collective-permute-start(f32[96,128]{1,0:T(8,128)S(1)} %get-tuple-element.28), channel_id=1, source_target_pairs={{0,240},{16,0},{32,16},{48,32},{64,48},{80,64},{96,80},{112,96},{1... | collective-permute-start | bytes 147464 | tf_op jit(solution)/shard_map/ppermute | solution.py:525
  36.8 31.4 %collective-permute-start.13 = (f32[688,128]{1,0:T(8,128)S(1)}, f32[688,128]{1,0:T(8,128)S(1)}, u32[]{:S(2)}, u32[]{:S(2)}) collective-permute-start(f32[688,128]{1,0:T(8,128)S(1)} %shard_map.137.near), channel_id=1, source_target_pairs={{0,1},{1,0},{2,3},{3,2},{4,5},{5,4},{6,7},{7,6},{8,9},{9,8},{10,11... | collective-permute-start | bytes 1056776 | tf_op jit(solution)/shard_map/ppermute | solution.py:525
  40.6 1.3 %collective-permute-start.7 = (f32[48,128]{1,0:T(8,128)S(1)}, f32[48,128]{1,0:T(8,128)S(1)}, u32[]{:S(2)}, u32[]{:S(2)}) collective-permute-start(f32[48,128]{1,0:T(8,128)S(1)} %get-tuple-element.29), channel_id=1, source_target_pairs={{0,1},{1,0},{2,3},{3,2},{4,5},{5,4},{6,7},{7,6},{8,9},{9,8},{10,11... | collective-permute-start | bytes 73736 | tf_op jit(solution)/shard_map/ppermute | solution.py:525
  62.4 6.9 %collective-permute-start.8 = (f32[96,128]{1,0:T(8,128)S(1)}, f32[96,128]{1,0:T(8,128)S(1)}, u32[]{:S(2)}, u32[]{:S(2)}) collective-permute-start(f32[96,128]{1,0:T(8,128)S(1)} %shard_map.135.own), channel_id=1, source_target_pairs={{0,1},{1,0},{2,3},{3,2},{4,5},{5,4},{6,7},{7,6},{8,9},{9,8},{10,11... | collective-permute-start | bytes 147464 | tf_op jit(solution)/shard_map/ppermute | solution.py:525
  68.1 1.2 %collective-permute-start.14 = (f32[32,128]{1,0:T(8,128)S(1)}, f32[32,128]{1,0:T(8,128)S(1)}, u32[]{:S(2)}, u32[]{:S(2)}) collective-permute-start(f32[32,128]{1,0:T(8,128)S(1)} %get-tuple-element.36.tips), channel_id=1, source_target_pairs={{0,1},{1,0},{2,3},{3,2},{4,5},{5,4},{6,7},{7,6},{8,9},{9,8},{10,11... | collective-permute-start | bytes 49160 | tf_op jit(solution)/shard_map/ppermute | solution.py:525

commit v2 on v1

--- a/solution.py
+++ b/solution.py
@@ -56,20 +56,14 @@
     basis_in, pressure_in, trans_y_in, coarse_off_in, coarse_diag_in, wo, wz, to_next_y, to_prev_y, coarse,
     basis, pressure, trans_y, coarse_off, coarse_diag, done,
 ):
-    copies = [
-        pltpu.make_async_copy(source, target, done.at[n])
-        for n, (source, target) in enumerate(
-            (
-                (basis_in, basis),
-                (coarse_off_in, coarse_off),
-                (coarse_diag_in, coarse_diag),
-                (pressure_in, pressure),
-                (trans_y_in, trans_y),
-            )
-        )
-    ]
-    for copy in copies:
-        copy.start()
+    def copy(n, source, target):
+        return pltpu.make_async_copy(source, target, done.at[n])
+
+    small = (copy(0, coarse_off_in, coarse_off), copy(1, coarse_diag_in, coarse_diag))
+    tiles = copy(2, basis_in, basis)
+    fields = (copy(3, pressure_in, pressure), copy(4, trans_y_in, trans_y))
+    for each in (*small, tiles, *fields):
+        each.start()
     core = lax.axis_index("gz")
     block = iota((32, 128), 0)
     lane = iota((32, 128), 1)
@@ -77,24 +71,8 @@
     def place(mask):
         return jnp.where(mask, 1.0, 0.0).astype(BF16)
 
-    for copy in copies:
-        copy.wait()
-    total = dot(basis[1], place(lane == 4 * block))
-    for k in (2, 3, 4):
-        total = total + dot(basis[k], place(lane == 4 * block + (k - 1)))
-    wo[...] = total
-    wz[...] = dot(basis[5], place((lane == 4 * block + 4) | ((block == 31) & (lane == 1) & (core == 0)))) + dot(
-        basis[0], place((lane == 4 * block - 1) | ((block == 0) & (lane == 1) & (core == 1)))
-    )
-    for n in range(2):
-        for half, w in enumerate((wo, wz)):
-            spot = (2 * n + half) * 12
-            to_next_y[pl.ds(spot, 12), :] = w[pl.ds((10 + n) * 48 + 3, 12, stride=4), :]
-            to_prev_y[pl.ds(spot, 12), :] = w[pl.ds(n * 48, 12, stride=4), :]
-    for x in range(8):
-        to_next_y[pl.ds(48 + x, 1), :] = pressure[x, pl.ds(31, 1), :]
-        to_next_y[pl.ds(56 + x, 1), :] = trans_y[x, pl.ds(31, 1), :]
-        to_prev_y[pl.ds(48 + x, 1), :] = pressure[x, pl.ds(0, 1), :]
+    for each in small:
+        each.wait()
     inverse = damping / coarse_diag[0]
     total = jnp.zeros((26, 128), F32)
     line = jnp.zeros((1, 128), F32)
@@ -106,6 +84,24 @@
     coarse[...] = jnp.zeros_like(coarse)
     coarse[pl.ds(0, 26), :] = total
     coarse[pl.ds(26, 1), :] = line
+    tiles.wait()
+    reach = dot(basis[0], place((lane == 4 * block - 1) | ((block == 0) & (lane == 1) & (core == 1))))
+    total = dot(basis[1], place(lane == 4 * block))
+    for k in (2, 3, 4):
+        total = total + dot(basis[k], place(lane == 4 * block + (k - 1)))
+    wo[...] = total
+    wz[...] = reach + dot(basis[5], place((lane == 4 * block + 4) | ((block == 31) & (lane == 1) & (core == 0))))
+    for each in fields:
+        each.wait()
+    for n in range(2):
+        for half, w in enumerate((wo, wz)):
+            spot = (2 * n + half) * 12
+            to_next_y[pl.ds(spot, 12), :] = w[pl.ds((10 + n) * 48 + 3, 12, stride=4), :]
+            to_prev_y[pl.ds(spot, 12), :] = w[pl.ds(n * 48, 12, stride=4), :]
+    for x in range(8):
+        to_next_y[pl.ds(48 + x, 1), :] = pressure[x, pl.ds(31, 1), :]
+        to_next_y[pl.ds(56 + x, 1), :] = trans_y[x, pl.ds(31, 1), :]
+        to_prev_y[pl.ds(48 + x, 1), :] = pressure[x, pl.ds(0, 1), :]
     to_next_y[pl.ds(64, 32), :] = coarse[...]
     to_prev_y[pl.ds(56, 32), :] = coarse[...]
 
@@ -156,30 +152,35 @@
         ref[pl.ds(128, 96), :] = narrow(near[pl.ds(208, 96), :])
 
 
-def window_kernel(up, down, from_prev_x, own, from_next_x, near):
+def window_kernel(up, down, from_prev_x, own, from_next_x, near, rows):
     def wide(rows):
         rows = rows.astype(F32)
         at = iota(rows.shape, 0) % 32
         return rows + jnp.where(at == 26, pltpu.roll(rows, rows.shape[0] - 1, 0), 0.0)
 
-    for spot, ref in ((0, up), (680, down)):
-        near[pl.ds(spot, 8), :] = jnp.zeros((8, 128), F32)
-        outer = ref[pl.ds(0, 32), :].astype(F32)
-        for yc in range(3):
-            near[pl.ds(spot + yc, 1), :] = outer[8 * yc + 2 : 8 * yc + 3] + outer[8 * yc + 3 : 8 * yc + 4]
-    near[pl.ds(8, 96), :] = wide(up[pl.ds(32, 96), :])
-    near[pl.ds(104, 96), :] = wide(up[pl.ds(128, 96), :])
-    near[pl.ds(200, 96), :] = from_prev_x[pl.ds(208, 96), :]
-    near[pl.ds(296, 96), :] = own[pl.ds(208, 96), :]
-    near[pl.ds(392, 96), :] = from_next_x[pl.ds(208, 96), :]
-    near[pl.ds(488, 96), :] = wide(down[pl.ds(128, 96), :])
-    near[pl.ds(584, 96), :] = wide(down[pl.ds(32, 96), :])
+    rows[pl.ds(0, 96), :] = wide(up[pl.ds(32, 96), :])
+    rows[pl.ds(96, 96), :] = wide(up[pl.ds(128, 96), :])
+    rows[pl.ds(192, 96), :] = from_prev_x[pl.ds(208, 96), :]
+    rows[pl.ds(288, 96), :] = own[pl.ds(208, 96), :]
+    rows[pl.ds(384, 96), :] = from_next_x[pl.ds(208, 96), :]
+    rows[pl.ds(480, 96), :] = wide(down[pl.ds(128, 96), :])
+    rows[pl.ds(576, 96), :] = wide(down[pl.ds(32, 96), :])
+    for yc in range(3):
+        for number in range(26):
+            near[pl.ds((yc * 26 + number) * 8, 7), :] = rows[pl.ds(yc * 32 + number, 7, stride=96), :]
+            near[pl.ds((yc * 26 + number) * 8 + 7, 1), :] = jnp.zeros((1, 128), F32)
+        spot = 624 + 16 * yc
+        near[pl.ds(spot + 8, 8), :] = jnp.zeros((8, 128), F32)
+        near[pl.ds(spot + 1, 7), :] = rows[pl.ds(yc * 32 + 26, 7, stride=96), :]
+        for at, ref in ((0, up), (8, down)):
+            outer = ref[pl.ds(0, 32), :].astype(F32)
+            near[pl.ds(spot + at, 1), :] = outer[8 * yc + 2 : 8 * yc + 3] + outer[8 * yc + 3 : 8 * yc + 4]
 
 
 def stack_kernel(near, far, coefs):
     core = lax.axis_index("gz")
-    coefs[pl.ds(pl.multiple_of(core * 688, 8), 688), :] = near[...]
-    coefs[pl.ds(pl.multiple_of((1 - core) * 688, 8), 688), :] = far[...]
+    coefs[pl.ds(pl.multiple_of(core * 672, 8), 672), :] = near[...]
+    coefs[pl.ds(pl.multiple_of((1 - core) * 672, 8), 672), :] = far[...]
 
 
 def wells_kernel(cells, rates, wells):
@@ -380,11 +381,7 @@
         valid = valid_x & (gy + yc - 1 >= 0) & (gy + yc - 1 < size_y)
         for zc in range(2):
             spot = (yc * 2 + zc) * 16
-            base = zc * 688
-            state[pl.ds(spot, 1), :] = coefs[pl.ds(base + yc, 1), :]
-            state[pl.ds(spot + 1, 7), :] = coefs[pl.ds(base + 8 + yc * 32 + 26, 7, stride=96), :]
-            state[pl.ds(spot + 8, 1), :] = coefs[pl.ds(base + 680 + yc, 1), :]
-            value = jnp.where(core == zc, mine, theirs) * state[pl.ds(spot, 9), :]
+            value = jnp.where(core == zc, mine, theirs) * coefs[pl.ds(zc * 672 + 624 + 16 * yc, 9), :]
             value = jnp.where(valid, value, 0.0)
             start[pl.ds(spot, 9), :] = value
             state[pl.ds(spot, 9), :] = value
@@ -427,7 +424,7 @@
                             if (a, b, c) == (0, 0, 0):
                                 continue
                             number = OFFSETS.index((a, b, c))
-                            coef = coefs[pl.ds(zc * 688 + 8 + yc * 32 + number, 7, stride=96), :]
+                            coef = coefs[pl.ds(zc * 672 + (yc * 26 + number) * 8, 7), :]
                             totals[yc, zc] = totals[yc, zc] - coef * values[b]
         for yc in range(3):
             valid = valid_x & (gy + yc - 1 >= 0) & (gy + yc - 1 < size_y)
@@ -573,15 +570,14 @@
     )(partial, pressure, trans_x, wo, wz, near_from_prev, near_from_next, from_prev_y, from_next_y, facing_y)
     shared = lax.all_to_all(message.reshape(count, 1, 256), ("gx", "gy"), 0, 0)
     shared = shared.reshape(2 * count, 128)
-
     tips, up, down = call(
         collect_kernel, [shape(32, 128), shape(224, 128, dtype=BF16), shape(224, 128, dtype=BF16)]
     )(from_prev_x, from_next_x, to_next_x)
     facing_x = shift(tips, "gz", 1)
-    near = call(window_kernel, shape(688, 128))(
+    near = call(window_kernel, shape(672, 128), [pltpu.VMEM((672, 128), F32)])(
         shift(up, "gx", 3), shift(down, "gx", -3), from_prev_x, to_next_x, from_next_x
     )
-    coefs = call(stack_kernel, shape(1376, 128))(near, shift(near, "gz", 1))
+    coefs = call(stack_kernel, shape(1344, 128))(near, shift(near, "gz", 1))
 
     own = call(gather_kernel, shape(96, 128), [pltpu.VMEM((576, 128), F32)])(shared)
     other = shift(own, "gz", 1)

time: 71.9 us -> 71.2 us (level)
  no operation moved by 1% of the time
where the time goes in v2:
time: 71.2 us; the launch traced here: 71 us
  starting transfers between devices  36.1 us (51%)
  blocking collectives  19.3 us (27%)
  waiting for transfers between devices  8.76 us (12%)
  Pallas kernels  6.07 us (9%)
  between operations  0.8 us (1%)
    ppermute x15, starting transfers between devices, shift(): lax.ppermute(value, axis, [(i, (i + steps) % count) for i in range(count)])  36.1 us
    all_to_all x1, blocking collectives, on_device(): shared = lax.all_to_all(message.reshape(count, 1, 256), ('gx', 'gy'), 0, 0)  19.3 us
    ppermute x15, waiting for transfers between devices, shift(): lax.ppermute(value, axis, [(i, (i + steps) % count) for i in range(count)])  8.76 us
    pallas_call x1, Pallas kernels, on_device(): call(solve_kernel, [shape(1, 4, 32), shape(8, 32, 128)], [pltpu.VMEM((96,...  1.87 us
    pallas_call x1, Pallas kernels, on_device(): call(pack_kernel, [shape(576, 128), shape(576, 128), shape(96, 128), shap...  1.76 us
  transfers between devices with their start and end apart: 15, of which 4 were waited for; matrix products, arithmetic and copies ran while one was open for 0% of the time, Pallas kernels for 3%

profile of v2, /device:TPU:1, one launch (start us, length us, event | category | flops | bytes accessed | tf_op | source)
XLA Modules:
  0.0 71.0 jit_solution(1457661784960232744)
XLA Ops:
  0.6 0.0 copy-start
  0.6 0.0 copy-start.4
  0.7 0.0 copy-start.6
  0.7 0.0 copy-start.7
  0.7 0.0 copy-start.2
  0.7 0.0 copy-start.3
  0.7 1.8 %shard_map.131 = (f32[576,128]{1,0:T(8,128)S(1)}, f32[576,128]{1,0:T(8,128)S(1)}, f32[96,128]{1,0:T(8,128)S(1)}, f32[88,128]{1,0:T(8,128)S(1)}, f32[32,128]{1,0:T(8,128)S(1)}) custom-call(bf16[6,576,32]{2,1,0:T(8,128)(2,1)} %bitcast.9, f32[8,32,128]{2,1,0:T(8,128)} %pressure.7, f32[8,32,128]{2,1,0:T(8,128)} %trans_y.1, f32[26,1,4,32]{3,2,1,0:T(4,128)} %coarse_off_in.1, ...), custom_call_target="tpu_custom_call" | custom-call | tf_op jit(solution)/shard_map/pallas_call | solution.py:528
  2.5 0.0 copy-start.1
  2.5 3.3 %collective-permute-start.4 = (f32[576,128]{1,0:T(8,128)S(1)}, f32[576,128]{1,0:T(8,128)S(1)}, u32[]{:S(2)}, u32[]{:S(2)}) collective-permute-start(f32[576,128]{1,0:T(8,128)S(1)} %get-tuple-element.24.wz), channel_id=1, source_target_pairs={{0,1},{1,0},{2,3},{3,2},{4,5},{5,4},{6,7},{7,6},{8,9},{9,8},{10,11... | collective-permute-start | bytes 884744 | tf_op jit(solution)/shard_map/ppermute | solution.py:522
  5.8 0.1 collective-permute-start
  5.9 0.4 collective-permute-start.1
  6.3 5.2 %collective-permute-start.2 = (f32[96,128]{1,0:T(8,128)S(1)}, f32[96,128]{1,0:T(8,128)S(1)}, u32[]{:S(2)}, u32[]{:S(2)}) collective-permute-start(f32[96,128]{1,0:T(8,128)S(1)} %get-tuple-element.21), channel_id=1, source_target_pairs={{0,2},{2,4},{4,6},{6,8},{8,10},{10,12},{12,14},{14,0},{1,3},{3,5},... | collective-permute-start | bytes 147464 | tf_op jit(solution)/shard_map/ppermute | solution.py:522
  11.5 2.5 %collective-permute-start.3 = (f32[88,128]{1,0:T(8,128)S(1)}, f32[88,128]{1,0:T(8,128)S(1)}, u32[]{:S(2)}, u32[]{:S(2)}) collective-permute-start(f32[88,128]{1,0:T(8,128)S(1)} %get-tuple-element.22), channel_id=1, source_target_pairs={{0,14},{2,0},{4,2},{6,4},{8,6},{10,8},{12,10},{14,12},{1,15},{3,1}... | collective-permute-start | bytes 135176 | tf_op jit(solution)/shard_map/ppermute | solution.py:522
  13.9 0.0 copy-done.7
  14.0 0.6 shard_map.130.wells
  14.5 3.9 %collective-permute-done.3.from_next_y = f32[88,128]{1,0:T(8,128)S(1)} collective-permute-done((f32[88,128]{1,0:T(8,128)S(1)}, f32[88,128]{1,0:T(8,128)S(1)}, u32[]{:S(2)}, u32[]{:S(2)}) %collective-permute-start.3) | collective-permute-done | bytes 45088 | tf_op jit(solution)/shard_map/ppermute | solution.py:522
  18.4 0.0 collective-permute-done.2.from_prev_y
  18.4 0.0 collective-permute-done.facing_p
  18.4 0.0 collective-permute-done.1.facing_t
  18.4 0.3 shard_map.132.partial
  18.7 0.0 collective-permute-done.4.facing
  18.7 0.2 shard_map.133
  18.9 1.3 %collective-permute-start.9 = (f32[304,128]{1,0:T(8,128)S(1)}, f32[304,128]{1,0:T(8,128)S(1)}, u32[]{:S(2)}, u32[]{:S(2)}) collective-permute-start(f32[304,128]{1,0:T(8,128)S(1)} %get-tuple-element.32.own), channel_id=1, source_target_pairs={{0,16},{16,32},{32,48},{48,64},{64,80},{80,96},{96,112},{112,128},... | collective-permute-start | bytes 466952 | tf_op jit(solution)/shard_map/ppermute | solution.py:522
  20.2 4.2 %collective-permute-start.10 = (f32[304,128]{1,0:T(8,128)S(1)}, f32[304,128]{1,0:T(8,128)S(1)}, u32[]{:S(2)}, u32[]{:S(2)}) collective-permute-start(f32[304,128]{1,0:T(8,128)S(1)} %get-tuple-element.33), channel_id=1, source_target_pairs={{0,240},{16,0},{32,16},{48,32},{64,48},{80,64},{96,80},{112,96},{1... | collective-permute-start | bytes 466952 | tf_op jit(solution)/shard_map/ppermute | solution.py:522
  24.4 2.6 %collective-permute-done.9.from_prev_x = f32[304,128]{1,0:T(8,128)S(1)} collective-permute-done((f32[304,128]{1,0:T(8,128)S(1)}, f32[304,128]{1,0:T(8,128)S(1)}, u32[]{:S(2)}, u32[]{:S(2)}) %collective-permute-start.9) | collective-permute-done | bytes 155680 | tf_op jit(solution)/shard_map/ppermute | solution.py:522
  27.0 0.0 collective-permute-done.10.from_next_x
  27.0 1.4 %collective-permute-start.11 = (bf16[224,128]{1,0:T(8,128)(2,1)S(1)}, bf16[224,128]{1,0:T(8,128)(2,1)S(1)}, u32[]{:S(2)}, u32[]{:S(2)}) collective-permute-start(bf16[224,128]{1,0:T(8,128)(2,1)S(1)} %get-tuple-element.34), channel_id=1, source_target_pairs={{0,48},{16,64},{32,80},{48,96},{64,112},{80,128},{96,144},{112,160... | collective-permute-start | bytes 172040 | tf_op jit(solution)/shard_map/ppermute | solution.py:522
  28.4 2.8 %collective-permute-start.12 = (bf16[224,128]{1,0:T(8,128)(2,1)S(1)}, bf16[224,128]{1,0:T(8,128)(2,1)S(1)}, u32[]{:S(2)}, u32[]{:S(2)}) collective-permute-start(bf16[224,128]{1,0:T(8,128)(2,1)S(1)} %get-tuple-element.35), channel_id=1, source_target_pairs={{0,208},{16,224},{32,240},{48,0},{64,16},{80,32},{96,48},{112,64},... | collective-permute-start | bytes 172040 | tf_op jit(solution)/shard_map/ppermute | solution.py:522
  31.2 0.0 collective-permute-start.5
  31.2 5.4 %collective-permute-start.6 = (f32[96,128]{1,0:T(8,128)S(1)}, f32[96,128]{1,0:T(8,128)S(1)}, u32[]{:S(2)}, u32[]{:S(2)}) collective-permute-start(f32[96,128]{1,0:T(8,128)S(1)} %get-tuple-element.28), channel_id=1, source_target_pairs={{0,240},{16,0},{32,16},{48,32},{64,48},{80,64},{96,80},{112,96},{1... | collective-permute-start | bytes 147464 | tf_op jit(solution)/shard_map/ppermute | solution.py:522
  36.6 0.0 collective-permute-done.11.up
  36.6 0.0 collective-permute-done.12.down
  36.6 0.2 shard_map.137.near
  36.9 3.8 %collective-permute-start.13 = (f32[672,128]{1,0:T(8,128)S(1)}, f32[672,128]{1,0:T(8,128)S(1)}, u32[]{:S(2)}, u32[]{:S(2)}) collective-permute-start(f32[672,128]{1,0:T(8,128)S(1)} %shard_map.137.near), channel_id=1, source_target_pairs={{0,1},{1,0},{2,3},{3,2},{4,5},{5,4},{6,7},{7,6},{8,9},{9,8},{10,11... | collective-permute-start | bytes 1032200 | tf_op jit(solution)/shard_map/ppermute | solution.py:522
  40.7 0.1 collective-permute-start.7
  40.8 1.2 %collective-permute-done.7.facing_y = f32[48,128]{1,0:T(8,128)S(1)} collective-permute-done((f32[48,128]{1,0:T(8,128)S(1)}, f32[48,128]{1,0:T(8,128)S(1)}, u32[]{:S(2)}, u32[]{:S(2)}) %collective-permute-start.7) | collective-permute-done | bytes 24608 | tf_op jit(solution)/shard_map/ppermute | solution.py:522
  42.0 0.0 collective-permute-done.6.near_from_next
  42.0 0.0 collective-permute-done.5.near_from_prev
  42.0 0.8 %shard_map.134 = (f32[8,32,128]{2,1,0:T(8,128)}, f32[256,128]{1,0:T(8,128)S(1)}) custom-call(f32[8,32,128]{2,1,0:T(8,128)S(1)} %shard_map.132.partial, f32[8,32,128]{2,1,0:T(8,128)S(1)} %copy-done, f32[8,32,128]{2,1,0:T(8,128)S(1)} %copy-done.1, f32[576,128]{1,0:T(8,128)S(1)} %get-tuple-element.23.wo, f32[576,128]{1,0:T(8,128)S(1)} %get-tuple-element.26.wz, ...), custom_call_target="tpu_custom_call" | custom-call | tf_op jit(solution)/shard_map/pallas_call | solution.py:566
  42.8 19.3 %all_to_all.5 = f32[128,1,256]{2,1,0:T(1,128)S(1)} all-to-all(f32[128,1,256]{2,1,0:T(1,128)S(1)} %bitcast.6), channel_id=1, replica_groups=mesh['gx'=16,'gy'=8,'gz'=2] {'gx','gy'}, dimensions={0} | all-to-all | bytes 262144 | tf_op jit(solution)/shard_map/all_to_all | solution.py:571
  62.1 0.3 shard_map.135.own
  62.4 5.6 %collective-permute-start.8 = (f32[96,128]{1,0:T(8,128)S(1)}, f32[96,128]{1,0:T(8,128)S(1)}, u32[]{:S(2)}, u32[]{:S(2)}) collective-permute-start(f32[96,128]{1,0:T(8,128)S(1)} %shard_map.135.own), channel_id=1, source_target_pairs={{0,1},{1,0},{2,3},{3,2},{4,5},{5,4},{6,7},{7,6},{8,9},{9,8},{10,11... | collective-permute-start | bytes 147464 | tf_op jit(solution)/shard_map/ppermute | solution.py:522
  68.0 0.1 collective-permute-start.14
  68.1 0.0 collective-permute-done.13.far
  68.1 0.1 shard_map.138.coefs
  68.1 1.0 %collective-permute-done.14.facing_x = f32[32,128]{1,0:T(8,128)S(1)} collective-permute-done((f32[32,128]{1,0:T(8,128)S(1)}, f32[32,128]{1,0:T(8,128)S(1)}, u32[]{:S(2)}, u32[]{:S(2)}) %collective-permute-start.14) | collective-permute-done | bytes 16416 | tf_op jit(solution)/shard_map/ppermute | solution.py:522
  69.2 0.0 collective-permute-done.8.other
  69.2 1.9 %shard_map.139 = (f32[1,4,32]{2,1,0:T(4,128)}, f32[8,32,128]{2,1,0:T(8,128)}) custom-call(f32[96,128]{1,0:T(8,128)S(1)} %shard_map.135.own, f32[96,128]{1,0:T(8,128)S(1)} %collective-permute-done.8.other, f32[1344,128]{1,0:T(8,128)S(1)} %shard_map.138.coefs, f32[576,128]{1,0:T(8,128)S(1)} %get-tuple-element.23.wo, f32[576,128]{1,0:T(8,128)S(1)} %get-tuple-element.26.wz, ...), custom_call_target="tpu_custom_call" | custom-call | tf_op jit(solution)/shard_map/pallas_call | solution.py:584
  (9 shorter events, 0.0 us)
Async XLA Ops:
  0.6 5.1 %copy-start = (f32[8,32,128]{2,1,0:T(8,128)S(1)}, f32[8,32,128]{2,1,0:T(8,128)}, u32[]{:S(2)}) copy-start(f32[8,32,128]{2,1,0:T(8,128)} %pressure.7) | copy-start | bytes 393220
  0.6 5.2 %copy-start.4 = (f32[8,32,128]{2,1,0:T(8,128)S(1)}, f32[8,32,128]{2,1,0:T(8,128)}, u32[]{:S(2)}) copy-start(f32[8,32,128]{2,1,0:T(8,128)} %trans_z.1) | copy-start | bytes 393220
  0.7 13.3 %copy-start.6 = (s32[1024]{0:T(1024)S(1)}, s32[1024]{0:T(1024)}, u32[]{:S(2)}) copy-start(s32[1024]{0:T(1024)} %param.17) | copy-start | bytes 12292
  0.7 13.3 %copy-start.7 = (f32[1024]{0:T(1024)S(1)}, f32[1024]{0:T(1024)}, u32[]{:S(2)}) copy-start(f32[1024]{0:T(1024)} %param.18) | copy-start | bytes 12292
  0.7 17.7 %copy-start.2 = (f32[8,32,128]{2,1,0:T(8,128)S(1)}, f32[8,32,128]{2,1,0:T(8,128)}, u32[]{:S(2)}) copy-start(f32[8,32,128]{2,1,0:T(8,128)} %trans_y.1) | copy-start | bytes 393220
  0.7 17.7 %copy-start.3 = (f32[8,32,128]{2,1,0:T(8,128)S(1)}, f32[8,32,128]{2,1,0:T(8,128)}, u32[]{:S(2)}) copy-start(f32[8,32,128]{2,1,0:T(8,128)} %accumulation.1) | copy-start | bytes 393220
  0.7 17.7 %copy-start.5 = (f32[8,32,128]{2,1,0:T(8,128)S(1)}, f32[8,32,128]{2,1,0:T(8,128)}, u32[]{:S(2)}) copy-start(f32[8,32,128]{2,1,0:T(8,128)} %source.1) | copy-start | bytes 393220
  2.5 16.0 %copy-start.1 = (f32[8,32,128]{2,1,0:T(8,128)S(1)}, f32[8,32,128]{2,1,0:T(8,128)}, u32[]{:S(2)}) copy-start(f32[8,32,128]{2,1,0:T(8,128)} %trans_x.5) | copy-start | bytes 393220
  2.5 16.3 %collective-permute-start.4 = (f32[576,128]{1,0:T(8,128)S(1)}, f32[576,128]{1,0:T(8,128)S(1)}, u32[]{:S(2)}, u32[]{:S(2)}) collective-permute-start(f32[576,128]{1,0:T(8,128)S(1)} %get-tuple-element.24.wz), channel_id=1, source_target_pairs={{0,1},{1,0},{2,3},{3,2},{4,5},{5,4},{6,7},{7,6},{8,9},{9,8},{10,11... | collective-permute-start | bytes 884744 | tf_op jit(solution)/shard_map/ppermute | solution.py:522
  5.8 12.6 %collective-permute-start = (f32[8,32,128]{2,1,0:T(8,128)S(1)}, f32[8,32,128]{2,1,0:T(8,128)S(1)}, u32[]{:S(2)}, u32[]{:S(2)}) collective-permute-start(f32[8,32,128]{2,1,0:T(8,128)S(1)} %copy-done), channel_id=1, source_target_pairs={{0,1},{1,0},{2,3},{3,2},{4,5},{5,4},{6,7},{7,6},{8,9},{9,8},{10,11... | collective-permute-start | bytes 393224 | tf_op jit(solution)/shard_map/ppermute | solution.py:522
  5.9 12.5 %collective-permute-start.1 = (f32[8,32,128]{2,1,0:T(8,128)S(1)}, f32[8,32,128]{2,1,0:T(8,128)S(1)}, u32[]{:S(2)}, u32[]{:S(2)}) collective-permute-start(f32[8,32,128]{2,1,0:T(8,128)S(1)} %copy-done.4), channel_id=1, source_target_pairs={{0,1},{1,0},{2,3},{3,2},{4,5},{5,4},{6,7},{7,6},{8,9},{9,8},{10,11... | collective-permute-start | bytes 393224 | tf_op jit(solution)/shard_map/ppermute | solution.py:522
  6.3 12.1 %collective-permute-start.2 = (f32[96,128]{1,0:T(8,128)S(1)}, f32[96,128]{1,0:T(8,128)S(1)}, u32[]{:S(2)}, u32[]{:S(2)}) collective-permute-start(f32[96,128]{1,0:T(8,128)S(1)} %get-tuple-element.21), channel_id=1, source_target_pairs={{0,2},{2,4},{4,6},{6,8},{8,10},{10,12},{12,14},{14,0},{1,3},{3,5},... | collective-permute-start | bytes 147464 | tf_op jit(solution)/shard_map/ppermute | solution.py:522
  11.5 6.9 %collective-permute-start.3 = (f32[88,128]{1,0:T(8,128)S(1)}, f32[88,128]{1,0:T(8,128)S(1)}, u32[]{:S(2)}, u32[]{:S(2)}) collective-permute-start(f32[88,128]{1,0:T(8,128)S(1)} %get-tuple-element.22), channel_id=1, source_target_pairs={{0,14},{2,0},{4,2},{6,4},{8,6},{10,8},{12,10},{14,12},{1,15},{3,1}... | collective-permute-start | bytes 135176 | tf_op jit(solution)/shard_map/ppermute | solution.py:522
  18.9 8.1 %collective-permute-start.9 = (f32[304,128]{1,0:T(8,128)S(1)}, f32[304,128]{1,0:T(8,128)S(1)}, u32[]{:S(2)}, u32[]{:S(2)}) collective-permute-start(f32[304,128]{1,0:T(8,128)S(1)} %get-tuple-element.32.own), channel_id=1, source_target_pairs={{0,16},{16,32},{32,48},{48,64},{64,80},{80,96},{96,112},{112,128},... | collective-permute-start | bytes 466952 | tf_op jit(solution)/shard_map/ppermute | solution.py:522
  20.2 6.8 %collective-permute-start.10 = (f32[304,128]{1,0:T(8,128)S(1)}, f32[304,128]{1,0:T(8,128)S(1)}, u32[]{:S(2)}, u32[]{:S(2)}) collective-permute-start(f32[304,128]{1,0:T(8,128)S(1)} %get-tuple-element.33), channel_id=1, source_target_pairs={{0,240},{16,0},{32,16},{48,32},{64,48},{80,64},{96,80},{112,96},{1... | collective-permute-start | bytes 466952 | tf_op jit(solution)/shard_map/ppermute | solution.py:522
  27.0 9.6 %collective-permute-start.11 = (bf16[224,128]{1,0:T(8,128)(2,1)S(1)}, bf16[224,128]{1,0:T(8,128)(2,1)S(1)}, u32[]{:S(2)}, u32[]{:S(2)}) collective-permute-start(bf16[224,128]{1,0:T(8,128)(2,1)S(1)} %get-tuple-element.34), channel_id=1, source_target_pairs={{0,48},{16,64},{32,80},{48,96},{64,112},{80,128},{96,144},{112,160... | collective-permute-start | bytes 172040 | tf_op jit(solution)/shard_map/ppermute | solution.py:522
  28.4 8.2 %collective-permute-start.12 = (bf16[224,128]{1,0:T(8,128)(2,1)S(1)}, bf16[224,128]{1,0:T(8,128)(2,1)S(1)}, u32[]{:S(2)}, u32[]{:S(2)}) collective-permute-start(bf16[224,128]{1,0:T(8,128)(2,1)S(1)} %get-tuple-element.35), channel_id=1, source_target_pairs={{0,208},{16,224},{32,240},{48,0},{64,16},{80,32},{96,48},{112,64},... | collective-permute-start | bytes 172040 | tf_op jit(solution)/shard_map/ppermute | solution.py:522
  31.2 10.7 %collective-permute-start.5 = (f32[128,128]{1,0:T(8,128)S(1)}, f32[128,128]{1,0:T(8,128)S(1)}, u32[]{:S(2)}, u32[]{:S(2)}) collective-permute-start(f32[128,128]{1,0:T(8,128)S(1)} %get-tuple-element.27), channel_id=1, source_target_pairs={{0,16},{16,32},{32,48},{48,64},{64,80},{80,96},{96,112},{112,128},... | collective-permute-start | bytes 196616 | tf_op jit(solution)/shard_map/ppermute | solution.py:522
  31.2 10.7 %collective-permute-start.6 = (f32[96,128]{1,0:T(8,128)S(1)}, f32[96,128]{1,0:T(8,128)S(1)}, u32[]{:S(2)}, u32[]{:S(2)}) collective-permute-start(f32[96,128]{1,0:T(8,128)S(1)} %get-tuple-element.28), channel_id=1, source_target_pairs={{0,240},{16,0},{32,16},{48,32},{64,48},{80,64},{96,80},{112,96},{1... | collective-permute-start | bytes 147464 | tf_op jit(solution)/shard_map/ppermute | solution.py:522
  36.9 31.2 %collective-permute-start.13 = (f32[672,128]{1,0:T(8,128)S(1)}, f32[672,128]{1,0:T(8,128)S(1)}, u32[]{:S(2)}, u32[]{:S(2)}) collective-permute-start(f32[672,128]{1,0:T(8,128)S(1)} %shard_map.137.near), channel_id=1, source_target_pairs={{0,1},{1,0},{2,3},{3,2},{4,5},{5,4},{6,7},{7,6},{8,9},{9,8},{10,11... | collective-permute-start | bytes 1032200 | tf_op jit(solution)/shard_map/ppermute | solution.py:522
  40.7 1.3 %collective-permute-start.7 = (f32[48,128]{1,0:T(8,128)S(1)}, f32[48,128]{1,0:T(8,128)S(1)}, u32[]{:S(2)}, u32[]{:S(2)}) collective-permute-start(f32[48,128]{1,0:T(8,128)S(1)} %get-tuple-element.29), channel_id=1, source_target_pairs={{0,1},{1,0},{2,3},{3,2},{4,5},{5,4},{6,7},{7,6},{8,9},{9,8},{10,11... | collective-permute-start | bytes 73736 | tf_op jit(solution)/shard_map/ppermute | solution.py:522
  62.4 6.7 %collective-permute-start.8 = (f32[96,128]{1,0:T(8,128)S(1)}, f32[96,128]{1,0:T(8,128)S(1)}, u32[]{:S(2)}, u32[]{:S(2)}) collective-permute-start(f32[96,128]{1,0:T(8,128)S(1)} %shard_map.135.own), channel_id=1, source_target_pairs={{0,1},{1,0},{2,3},{3,2},{4,5},{5,4},{6,7},{7,6},{8,9},{9,8},{10,11... | collective-permute-start | bytes 147464 | tf_op jit(solution)/shard_map/ppermute | solution.py:522
  68.0 1.2 %collective-permute-start.14 = (f32[32,128]{1,0:T(8,128)S(1)}, f32[32,128]{1,0:T(8,128)S(1)}, u32[]{:S(2)}, u32[]{:S(2)}) collective-permute-start(f32[32,128]{1,0:T(8,128)S(1)} %get-tuple-element.36.tips), channel_id=1, source_target_pairs={{0,1},{1,0},{2,3},{3,2},{4,5},{5,4},{6,7},{7,6},{8,9},{9,8},{10,11... | collective-permute-start | bytes 49160 | tf_op jit(solution)/shard_map/ppermute | solution.py:522

commit v3 on v2

--- a/solution.py
+++ b/solution.py
@@ -52,25 +52,50 @@
     return mine + jnp.where(lane == 127 - 127 * core, pltpu.roll(theirs, 126 + core, 1), 0.0)
 
 
-def pack_kernel(
-    basis_in, pressure_in, trans_y_in, coarse_off_in, coarse_diag_in, wo, wz, to_next_y, to_prev_y, coarse,
-    basis, pressure, trans_y, coarse_off, coarse_diag, done,
+def place(mask):
+    return jnp.where(mask, 1.0, 0.0).astype(BF16)
+
+
+def spread_tiles(core, basis):
+    block = iota((32, 128), 0)
+    lane = iota((32, 128), 1)
+    inner = dot(basis[1], place(lane == 4 * block))
+    for k in (2, 3, 4):
+        inner = inner + dot(basis[k], place(lane == 4 * block + (k - 1)))
+    outer = dot(basis[5], place((lane == 4 * block + 4) | ((block == 31) & (lane == 1) & (core == 0)))) + dot(
+        basis[0], place((lane == 4 * block - 1) | ((block == 0) & (lane == 1) & (core == 1)))
+    )
+    return inner, outer
+
+
+def pack_kernel(basis_in, wo, wz, basis, done):
+    copy = pltpu.make_async_copy(basis_in, basis, done)
+    copy.start()
+    copy.wait()
+    inner, outer = spread_tiles(lax.axis_index("gz"), basis)
+    wo[...] = inner
+    wz[...] = outer
+
+
+def front_kernel(
+    basis_in, pressure_in, trans_y_in, coarse_off_in, coarse_diag_in, to_next_y, to_prev_y, coarse,
+    basis, pressure, trans_y, coarse_off, coarse_diag, wo, wz, done,
 ):
     def copy(n, source, target):
         return pltpu.make_async_copy(source, target, done.at[n])
 
     small = (copy(0, coarse_off_in, coarse_off), copy(1, coarse_diag_in, coarse_diag))
-    tiles = copy(2, basis_in, basis)
-    fields = (copy(3, pressure_in, pressure), copy(4, trans_y_in, trans_y))
-    for each in (*small, tiles, *fields):
+    large = (
+        copy(2, basis_in.at[:, pl.ds(0, 96)], basis.at[:, pl.ds(0, 96)]),
+        copy(3, basis_in.at[:, pl.ds(480, 96)], basis.at[:, pl.ds(96, 96)]),
+        copy(4, pressure_in, pressure),
+        copy(5, trans_y_in, trans_y),
+    )
+    for each in (*small, *large):
         each.start()
     core = lax.axis_index("gz")
     block = iota((32, 128), 0)
     lane = iota((32, 128), 1)
-
-    def place(mask):
-        return jnp.where(mask, 1.0, 0.0).astype(BF16)
-
     for each in small:
         each.wait()
     inverse = damping / coarse_diag[0]
@@ -84,19 +109,15 @@
     coarse[...] = jnp.zeros_like(coarse)
     coarse[pl.ds(0, 26), :] = total
     coarse[pl.ds(26, 1), :] = line
-    tiles.wait()
-    reach = dot(basis[0], place((lane == 4 * block - 1) | ((block == 0) & (lane == 1) & (core == 1))))
-    total = dot(basis[1], place(lane == 4 * block))
-    for k in (2, 3, 4):
-        total = total + dot(basis[k], place(lane == 4 * block + (k - 1)))
-    wo[...] = total
-    wz[...] = reach + dot(basis[5], place((lane == 4 * block + 4) | ((block == 31) & (lane == 1) & (core == 0))))
-    for each in fields:
+    for each in large:
         each.wait()
+    inner, outer = spread_tiles(core, basis)
+    wo[...] = inner
+    wz[...] = outer
     for n in range(2):
         for half, w in enumerate((wo, wz)):
             spot = (2 * n + half) * 12
-            to_next_y[pl.ds(spot, 12), :] = w[pl.ds((10 + n) * 48 + 3, 12, stride=4), :]
+            to_next_y[pl.ds(spot, 12), :] = w[pl.ds((2 + n) * 48 + 3, 12, stride=4), :]
             to_prev_y[pl.ds(spot, 12), :] = w[pl.ds(n * 48, 12, stride=4), :]
     for x in range(8):
         to_next_y[pl.ds(48 + x, 1), :] = pressure[x, pl.ds(31, 1), :]
@@ -525,26 +546,33 @@
 def on_device(
     pressure, accumulation, trans_x, trans_y, trans_z, source, well_cells, well_rates, basis, coarse_off, coarse_diag
 ):
-    wo, wz, to_next_y, to_prev_y, coarse = call(
-        pack_kernel,
-        [shape(576, 128), shape(576, 128), shape(96, 128), shape(88, 128), shape(32, 128)],
+    tiles, *others = (
+        pltpu.with_memory_space_constraint(operand, pltpu.HBM)
+        for operand in (basis.reshape(6, 576, 32), pressure, trans_y, coarse_off, coarse_diag)
+    )
+    to_next_y, to_prev_y, coarse = call(
+        front_kernel,
+        [shape(96, 128), shape(88, 128), shape(32, 128)],
         [
-            pltpu.VMEM((6, 576, 32), BF16),
+            pltpu.VMEM((6, 192, 32), BF16),
             pltpu.VMEM((8, 32, 128), F32),
             pltpu.VMEM((8, 32, 128), F32),
             pltpu.VMEM((26, 1, 4, 32), F32),
             pltpu.VMEM((1, 4, 32), F32),
-            pltpu.SemaphoreType.DMA((5,)),
+            pltpu.VMEM((192, 128), F32),
+            pltpu.VMEM((192, 128), F32),
+            pltpu.SemaphoreType.DMA((6,)),
         ],
         in_specs=[pl.BlockSpec(memory_space=pltpu.HBM)] * 5,
-    )(
-        *(
-            pltpu.with_memory_space_constraint(operand, pltpu.HBM)
-            for operand in (basis.reshape(6, 576, 32), pressure, trans_y, coarse_off, coarse_diag)
-        )
-    )
+    )(tiles, *others)
     from_prev_y = shift(to_next_y, "gy", 1)
     from_next_y = shift(to_prev_y, "gy", -1)
+    wo, wz = call(
+        pack_kernel,
+        [shape(576, 128), shape(576, 128)],
+        [pltpu.VMEM((6, 576, 32), BF16), pltpu.SemaphoreType.DMA],
+        in_specs=[pl.BlockSpec(memory_space=pltpu.HBM)],
+    )(tiles)
     facing = shift(wz, "gz", 1)
     facing_p = shift(pressure, "gz", 1)
     facing_t = shift(trans_z, "gz", 1)

time: 71.2 us -> 76.2 us (1.070)
  Pallas kernels: 6.07 us -> 11 us
    pallas_call x1 -> x2, Pallas kernels: 1.76 us -> 3.08 us  [the longest x1 1.58 us: on_device(): call(pack_kernel, [shape(576, 128), shape(576, 128)], [pltpu.VMEM((6, 576...]
    pallas_call x1, Pallas kernels: 0.15 us -> 1.07 us  [on_device(): call(relay_kernel, [shape(576, 128), shape(128, 128), shape(96, 128), sha...]
    pallas_call x1, Pallas kernels: 1.87 us -> 2.78 us  [on_device(): call(solve_kernel, [shape(1, 4, 32), shape(8, 32, 128)], [pltpu.VMEM((96,...]
    pallas_call x1, Pallas kernels: 0.28 us -> 1.18 us  [on_device(): call(local_kernel, shape(8, 32, 128))]
    pallas_call x1, Pallas kernels: 0.82 us -> 1.65 us  [on_device(): call(sums_kernel, [shape(8, 32, 128), shape(2 * count, 128)], [pltpu.VMEM...]
  transfers between devices with their start and end apart: 15 -> 15, of which waited for: 4 -> 4; matrix products, arithmetic and copies ran while one was open for 0% -> 0% of each run, Pallas kernels for 3% -> 7%
where the time goes in v3:
time: 76.2 us; the launch traced here: 76 us
  starting transfers between devices  36.2 us (48%)
  blocking collectives  19.3 us (25%)
  Pallas kernels  11 us (14%)
  waiting for transfers between devices  8.67 us (11%)
  between operations  0.77 us (1%)
    ppermute x15, starting transfers between devices, shift(): lax.ppermute(value, axis, [(i, (i + steps) % count) for i in range(count)])  36.2 us
    all_to_all x1, blocking collectives, on_device(): shared = lax.all_to_all(message.reshape(count, 1, 256), ('gx', 'gy'), 0, 0)  19.3 us
    ppermute x15, waiting for transfers between devices, shift(): lax.ppermute(value, axis, [(i, (i + steps) % count) for i in range(count)])  8.67 us
    pallas_call x1, Pallas kernels, on_device(): call(solve_kernel, [shape(1, 4, 32), shape(8, 32, 128)], [pltpu.VMEM((96,...  2.78 us
    pallas_call x1, Pallas kernels, on_device(): call(sums_kernel, [shape(8, 32, 128), shape(2 * count, 128)], [pltpu.VMEM...  1.65 us
    pallas_call x1, Pallas kernels, on_device(): call(pack_kernel, [shape(576, 128), shape(576, 128)], [pltpu.VMEM((6, 576...  1.58 us
  transfers between devices with their start and end apart: 15, of which 4 were waited for; matrix products, arithmetic and copies ran while one was open for 0% of the time, Pallas kernels for 7%

profile of v3, /device:TPU:1, one launch (start us, length us, event | category | flops | bytes accessed | tf_op | source)
XLA Modules:
  0.0 76.0 jit_solution(4905274074382528185)
XLA Ops:
  0.6 0.0 copy-start.3
  0.6 1.6 %shard_map.133 = (f32[576,128]{1,0:T(8,128)S(1)}, f32[576,128]{1,0:T(8,128)S(1)}) custom-call(bf16[6,576,32]{2,1,0:T(8,128)(2,1)} %bitcast.9), custom_call_target="tpu_custom_call" | custom-call | tf_op jit(solution)/shard_map/pallas_call | solution.py:570
  2.2 3.3 %collective-permute-start.4 = (f32[576,128]{1,0:T(8,128)S(1)}, f32[576,128]{1,0:T(8,128)S(1)}, u32[]{:S(2)}, u32[]{:S(2)}) collective-permute-start(f32[576,128]{1,0:T(8,128)S(1)} %get-tuple-element.24.wz), channel_id=1, source_target_pairs={{0,1},{1,0},{2,3},{3,2},{4,5},{5,4},{6,7},{7,6},{8,9},{9,8},{10,11... | collective-permute-start | bytes 884744 | tf_op jit(solution)/shard_map/ppermute | solution.py:543
  5.5 0.1 collective-permute-start
  5.6 0.0 copy-done.3
  5.6 0.4 collective-permute-start.1
  6.0 0.0 copy-start.4
  6.1 1.5 %shard_map.131 = (f32[96,128]{1,0:T(8,128)S(1)}, f32[88,128]{1,0:T(8,128)S(1)}, f32[32,128]{1,0:T(8,128)S(1)}) custom-call(bf16[6,576,32]{2,1,0:T(8,128)(2,1)} %bitcast.10, f32[8,32,128]{2,1,0:T(8,128)} %pressure.7, f32[8,32,128]{2,1,0:T(8,128)} %trans_y.1, f32[26,1,4,32]{3,2,1,0:T(4,128)} %coarse_off_in.1, f32[1,4,32]{2,1,0:T(4,128)} %coarse_diag_in.1), custom_call_target="tpu_custom_call" | custom-call | tf_op jit(solution)/shard_map/pallas_call | solution.py:553
  7.6 0.0 copy-start
  7.6 5.3 %collective-permute-start.2 = (f32[96,128]{1,0:T(8,128)S(1)}, f32[96,128]{1,0:T(8,128)S(1)}, u32[]{:S(2)}, u32[]{:S(2)}) collective-permute-start(f32[96,128]{1,0:T(8,128)S(1)} %get-tuple-element.21), channel_id=1, source_target_pairs={{0,2},{2,4},{4,6},{6,8},{8,10},{10,12},{12,14},{14,0},{1,3},{3,5},... | collective-permute-start | bytes 147464 | tf_op jit(solution)/shard_map/ppermute | solution.py:543
  12.9 2.5 %collective-permute-start.3 = (f32[88,128]{1,0:T(8,128)S(1)}, f32[88,128]{1,0:T(8,128)S(1)}, u32[]{:S(2)}, u32[]{:S(2)}) collective-permute-start(f32[88,128]{1,0:T(8,128)S(1)} %get-tuple-element.22), channel_id=1, source_target_pairs={{0,14},{2,0},{4,2},{6,4},{8,6},{10,8},{12,10},{14,12},{1,15},{3,1}... | collective-permute-start | bytes 135176 | tf_op jit(solution)/shard_map/ppermute | solution.py:543
  15.4 0.0 copy-done.5
  15.4 0.0 copy-done.6
  15.4 0.6 shard_map.130.wells
  16.0 3.8 %collective-permute-done.3.from_next_y = f32[88,128]{1,0:T(8,128)S(1)} collective-permute-done((f32[88,128]{1,0:T(8,128)S(1)}, f32[88,128]{1,0:T(8,128)S(1)}, u32[]{:S(2)}, u32[]{:S(2)}) %collective-permute-start.3) | collective-permute-done | bytes 45088 | tf_op jit(solution)/shard_map/ppermute | solution.py:543
  19.8 0.0 collective-permute-done.2.from_prev_y
  19.8 0.0 collective-permute-done.facing_p
  19.8 0.0 collective-permute-done.1.facing_t
  19.8 0.0 copy-done.1
  19.8 1.2 %shard_map.132.partial = f32[8,32,128]{2,1,0:T(8,128)S(1)} custom-call(f32[8,32,128]{2,1,0:T(8,128)} %pressure.7, f32[8,32,128]{2,1,0:T(8,128)S(1)} %copy-done.2, f32[8,32,128]{2,1,0:T(8,128)S(1)} %copy-done, f32[8,32,128]{2,1,0:T(8,128)S(1)} %copy-done.1, f32[8,32,128]{2,1,0:T(8,128)S(1)} %copy-done.3, f32[8,32,128]{2,1,0:T(8,128)S(1)} %copy-done.4, ...), custom_call_target="tpu_custom_call" | custom-call | tf_op jit(solution)/shard_map/pallas_call | solution.py:580
  21.0 0.0 collective-permute-done.4.facing
  21.0 1.1 %shard_map.134 = (f32[576,128]{1,0:T(8,128)S(1)}, f32[128,128]{1,0:T(8,128)S(1)}, f32[96,128]{1,0:T(8,128)S(1)}, f32[304,128]{1,0:T(8,128)S(1)}, f32[304,128]{1,0:T(8,128)S(1)}, /*index=5*/f32[48,128]{1,0:T(8,128)S(1)}) custom-call(f32[576,128]{1,0:T(8,128)S(1)} %get-tuple-element.23.wo, f32[576,128]{1,0:T(8,128)S(1)} %get-tuple-element.24.wz, ...), custom_call_target="tpu_custom_call" | custom-call | tf_op jit(solution)/shard_map/pallas_call | solution.py:583
  22.1 1.3 %collective-permute-start.9 = (f32[304,128]{1,0:T(8,128)S(1)}, f32[304,128]{1,0:T(8,128)S(1)}, u32[]{:S(2)}, u32[]{:S(2)}) collective-permute-start(f32[304,128]{1,0:T(8,128)S(1)} %get-tuple-element.32.own), channel_id=1, source_target_pairs={{0,16},{16,32},{32,48},{48,64},{64,80},{80,96},{96,112},{112,128},... | collective-permute-start | bytes 466952 | tf_op jit(solution)/shard_map/ppermute | solution.py:543
  23.4 4.2 %collective-permute-start.10 = (f32[304,128]{1,0:T(8,128)S(1)}, f32[304,128]{1,0:T(8,128)S(1)}, u32[]{:S(2)}, u32[]{:S(2)}) collective-permute-start(f32[304,128]{1,0:T(8,128)S(1)} %get-tuple-element.33), channel_id=1, source_target_pairs={{0,240},{16,0},{32,16},{48,32},{64,48},{80,64},{96,80},{112,96},{1... | collective-permute-start | bytes 466952 | tf_op jit(solution)/shard_map/ppermute | solution.py:543
  27.5 2.6 %collective-permute-done.9.from_prev_x = f32[304,128]{1,0:T(8,128)S(1)} collective-permute-done((f32[304,128]{1,0:T(8,128)S(1)}, f32[304,128]{1,0:T(8,128)S(1)}, u32[]{:S(2)}, u32[]{:S(2)}) %collective-permute-start.9) | collective-permute-done | bytes 155680 | tf_op jit(solution)/shard_map/ppermute | solution.py:543
  30.2 0.0 collective-permute-done.10.from_next_x
  30.2 1.4 %collective-permute-start.11 = (bf16[224,128]{1,0:T(8,128)(2,1)S(1)}, bf16[224,128]{1,0:T(8,128)(2,1)S(1)}, u32[]{:S(2)}, u32[]{:S(2)}) collective-permute-start(bf16[224,128]{1,0:T(8,128)(2,1)S(1)} %get-tuple-element.34), channel_id=1, source_target_pairs={{0,48},{16,64},{32,80},{48,96},{64,112},{80,128},{96,144},{112,160... | collective-permute-start | bytes 172040 | tf_op jit(solution)/shard_map/ppermute | solution.py:543
  31.6 2.8 %collective-permute-start.12 = (bf16[224,128]{1,0:T(8,128)(2,1)S(1)}, bf16[224,128]{1,0:T(8,128)(2,1)S(1)}, u32[]{:S(2)}, u32[]{:S(2)}) collective-permute-start(bf16[224,128]{1,0:T(8,128)(2,1)S(1)} %get-tuple-element.35), channel_id=1, source_target_pairs={{0,208},{16,224},{32,240},{48,0},{64,16},{80,32},{96,48},{112,64},... | collective-permute-start | bytes 172040 | tf_op jit(solution)/shard_map/ppermute | solution.py:543
  34.4 0.0 collective-permute-start.5
  34.4 5.4 %collective-permute-start.6 = (f32[96,128]{1,0:T(8,128)S(1)}, f32[96,128]{1,0:T(8,128)S(1)}, u32[]{:S(2)}, u32[]{:S(2)}) collective-permute-start(f32[96,128]{1,0:T(8,128)S(1)} %get-tuple-element.28), channel_id=1, source_target_pairs={{0,240},{16,0},{32,16},{48,32},{64,48},{80,64},{96,80},{112,96},{1... | collective-permute-start | bytes 147464 | tf_op jit(solution)/shard_map/ppermute | solution.py:543
  39.8 0.0 collective-permute-done.11.up
  39.8 0.0 collective-permute-done.12.down
  39.8 0.2 shard_map.138.near
  40.0 3.8 %collective-permute-start.13 = (f32[672,128]{1,0:T(8,128)S(1)}, f32[672,128]{1,0:T(8,128)S(1)}, u32[]{:S(2)}, u32[]{:S(2)}) collective-permute-start(f32[672,128]{1,0:T(8,128)S(1)} %shard_map.138.near), channel_id=1, source_target_pairs={{0,1},{1,0},{2,3},{3,2},{4,5},{5,4},{6,7},{7,6},{8,9},{9,8},{10,11... | collective-permute-start | bytes 1032200 | tf_op jit(solution)/shard_map/ppermute | solution.py:543
  43.8 0.1 collective-permute-start.7
  43.9 1.2 %collective-permute-done.7.facing_y = f32[48,128]{1,0:T(8,128)S(1)} collective-permute-done((f32[48,128]{1,0:T(8,128)S(1)}, f32[48,128]{1,0:T(8,128)S(1)}, u32[]{:S(2)}, u32[]{:S(2)}) %collective-permute-start.7) | collective-permute-done | bytes 24608 | tf_op jit(solution)/shard_map/ppermute | solution.py:543
  45.1 0.0 collective-permute-done.6.near_from_next
  45.1 0.0 collective-permute-done.5.near_from_prev
  45.1 1.7 %shard_map.135 = (f32[8,32,128]{2,1,0:T(8,128)}, f32[256,128]{1,0:T(8,128)S(1)}) custom-call(f32[8,32,128]{2,1,0:T(8,128)S(1)} %shard_map.132.partial, f32[8,32,128]{2,1,0:T(8,128)} %pressure.7, f32[8,32,128]{2,1,0:T(8,128)S(1)} %copy-done, f32[576,128]{1,0:T(8,128)S(1)} %get-tuple-element.23.wo, f32[576,128]{1,0:T(8,128)S(1)} %get-tuple-element.26.wz, ...), custom_call_target="tpu_custom_call" | custom-call | tf_op jit(solution)/shard_map/pallas_call | solution.py:594
  46.8 19.3 %all_to_all.5 = f32[128,1,256]{2,1,0:T(1,128)S(1)} all-to-all(f32[128,1,256]{2,1,0:T(1,128)S(1)} %bitcast.6), channel_id=1, replica_groups=mesh['gx'=16,'gy'=8,'gz'=2] {'gx','gy'}, dimensions={0} | all-to-all | bytes 262144 | tf_op jit(solution)/shard_map/all_to_all | solution.py:599
  66.1 0.3 shard_map.136.own
  66.4 5.6 %collective-permute-start.8 = (f32[96,128]{1,0:T(8,128)S(1)}, f32[96,128]{1,0:T(8,128)S(1)}, u32[]{:S(2)}, u32[]{:S(2)}) collective-permute-start(f32[96,128]{1,0:T(8,128)S(1)} %shard_map.136.own), channel_id=1, source_target_pairs={{0,1},{1,0},{2,3},{3,2},{4,5},{5,4},{6,7},{7,6},{8,9},{9,8},{10,11... | collective-permute-start | bytes 147464 | tf_op jit(solution)/shard_map/ppermute | solution.py:543
  72.0 0.1 collective-permute-start.14
  72.1 0.0 collective-permute-done.13.far
  72.1 0.1 shard_map.139.coefs
  72.1 1.0 %collective-permute-done.14.facing_x = f32[32,128]{1,0:T(8,128)S(1)} collective-permute-done((f32[32,128]{1,0:T(8,128)S(1)}, f32[32,128]{1,0:T(8,128)S(1)}, u32[]{:S(2)}, u32[]{:S(2)}) %collective-permute-start.14) | collective-permute-done | bytes 16416 | tf_op jit(solution)/shard_map/ppermute | solution.py:543
  73.2 0.0 collective-permute-done.8.other
  73.2 2.8 %shard_map.140 = (f32[1,4,32]{2,1,0:T(4,128)}, f32[8,32,128]{2,1,0:T(8,128)}) custom-call(f32[96,128]{1,0:T(8,128)S(1)} %shard_map.136.own, f32[96,128]{1,0:T(8,128)S(1)} %collective-permute-done.8.other, f32[1344,128]{1,0:T(8,128)S(1)} %shard_map.139.coefs, f32[576,128]{1,0:T(8,128)S(1)} %get-tuple-element.23.wo, f32[576,128]{1,0:T(8,128)S(1)} %get-tuple-element.26.wz, ...), custom_call_target="tpu_custom_call" | custom-call | tf_op jit(solution)/shard_map/pallas_call | solution.py:612
  (8 shorter events, 0.0 us)
Async XLA Ops:
  0.6 5.0 %copy-start.3 = (f32[8,32,128]{2,1,0:T(8,128)S(1)}, f32[8,32,128]{2,1,0:T(8,128)}, u32[]{:S(2)}) copy-start(f32[8,32,128]{2,1,0:T(8,128)} %trans_z.1) | copy-start | bytes 393220
  2.2 18.8 %collective-permute-start.4 = (f32[576,128]{1,0:T(8,128)S(1)}, f32[576,128]{1,0:T(8,128)S(1)}, u32[]{:S(2)}, u32[]{:S(2)}) collective-permute-start(f32[576,128]{1,0:T(8,128)S(1)} %get-tuple-element.24.wz), channel_id=1, source_target_pairs={{0,1},{1,0},{2,3},{3,2},{4,5},{5,4},{6,7},{7,6},{8,9},{9,8},{10,11... | collective-permute-start | bytes 884744 | tf_op jit(solution)/shard_map/ppermute | solution.py:543
  5.5 14.2 %collective-permute-start = (f32[8,32,128]{2,1,0:T(8,128)}, f32[8,32,128]{2,1,0:T(8,128)S(1)}, u32[]{:S(2)}, u32[]{:S(2)}) collective-permute-start(f32[8,32,128]{2,1,0:T(8,128)} %pressure.7), channel_id=1, source_target_pairs={{0,1},{1,0},{2,3},{3,2},{4,5},{5,4},{6,7},{7,6},{8,9},{9,8},{10,11... | collective-permute-start | bytes 393224 | tf_op jit(solution)/shard_map/ppermute | solution.py:543
  5.6 14.1 %collective-permute-start.1 = (f32[8,32,128]{2,1,0:T(8,128)S(1)}, f32[8,32,128]{2,1,0:T(8,128)S(1)}, u32[]{:S(2)}, u32[]{:S(2)}) collective-permute-start(f32[8,32,128]{2,1,0:T(8,128)S(1)} %copy-done.3), channel_id=1, source_target_pairs={{0,1},{1,0},{2,3},{3,2},{4,5},{5,4},{6,7},{7,6},{8,9},{9,8},{10,11... | collective-permute-start | bytes 393224 | tf_op jit(solution)/shard_map/ppermute | solution.py:543
  6.0 9.4 %copy-start.5 = (s32[1024]{0:T(1024)S(1)}, s32[1024]{0:T(1024)}, u32[]{:S(2)}) copy-start(s32[1024]{0:T(1024)} %param.17) | copy-start | bytes 12292
  6.0 9.4 %copy-start.6 = (f32[1024]{0:T(1024)S(1)}, f32[1024]{0:T(1024)}, u32[]{:S(2)}) copy-start(f32[1024]{0:T(1024)} %param.18) | copy-start | bytes 12292
  6.0 13.7 %copy-start.1 = (f32[8,32,128]{2,1,0:T(8,128)S(1)}, f32[8,32,128]{2,1,0:T(8,128)}, u32[]{:S(2)}) copy-start(f32[8,32,128]{2,1,0:T(8,128)} %trans_y.1) | copy-start | bytes 393220
  6.0 13.7 %copy-start.2 = (f32[8,32,128]{2,1,0:T(8,128)S(1)}, f32[8,32,128]{2,1,0:T(8,128)}, u32[]{:S(2)}) copy-start(f32[8,32,128]{2,1,0:T(8,128)} %accumulation.1) | copy-start | bytes 393220
  6.0 13.7 %copy-start.4 = (f32[8,32,128]{2,1,0:T(8,128)S(1)}, f32[8,32,128]{2,1,0:T(8,128)}, u32[]{:S(2)}) copy-start(f32[8,32,128]{2,1,0:T(8,128)} %source.1) | copy-start | bytes 393220
  7.6 12.2 %copy-start = (f32[8,32,128]{2,1,0:T(8,128)S(1)}, f32[8,32,128]{2,1,0:T(8,128)}, u32[]{:S(2)}) copy-start(f32[8,32,128]{2,1,0:T(8,128)} %trans_x.5) | copy-start | bytes 393220
  7.6 12.2 %collective-permute-start.2 = (f32[96,128]{1,0:T(8,128)S(1)}, f32[96,128]{1,0:T(8,128)S(1)}, u32[]{:S(2)}, u32[]{:S(2)}) collective-permute-start(f32[96,128]{1,0:T(8,128)S(1)} %get-tuple-element.21), channel_id=1, source_target_pairs={{0,2},{2,4},{4,6},{6,8},{8,10},{10,12},{12,14},{14,0},{1,3},{3,5},... | collective-permute-start | bytes 147464 | tf_op jit(solution)/shard_map/ppermute | solution.py:543
  12.9 6.9 %collective-permute-start.3 = (f32[88,128]{1,0:T(8,128)S(1)}, f32[88,128]{1,0:T(8,128)S(1)}, u32[]{:S(2)}, u32[]{:S(2)}) collective-permute-start(f32[88,128]{1,0:T(8,128)S(1)} %get-tuple-element.22), channel_id=1, source_target_pairs={{0,14},{2,0},{4,2},{6,4},{8,6},{10,8},{12,10},{14,12},{1,15},{3,1}... | collective-permute-start | bytes 135176 | tf_op jit(solution)/shard_map/ppermute | solution.py:543
  22.1 8.1 %collective-permute-start.9 = (f32[304,128]{1,0:T(8,128)S(1)}, f32[304,128]{1,0:T(8,128)S(1)}, u32[]{:S(2)}, u32[]{:S(2)}) collective-permute-start(f32[304,128]{1,0:T(8,128)S(1)} %get-tuple-element.32.own), channel_id=1, source_target_pairs={{0,16},{16,32},{32,48},{48,64},{64,80},{80,96},{96,112},{112,128},... | collective-permute-start | bytes 466952 | tf_op jit(solution)/shard_map/ppermute | solution.py:543
  23.4 6.8 %collective-permute-start.10 = (f32[304,128]{1,0:T(8,128)S(1)}, f32[304,128]{1,0:T(8,128)S(1)}, u32[]{:S(2)}, u32[]{:S(2)}) collective-permute-start(f32[304,128]{1,0:T(8,128)S(1)} %get-tuple-element.33), channel_id=1, source_target_pairs={{0,240},{16,0},{32,16},{48,32},{64,48},{80,64},{96,80},{112,96},{1... | collective-permute-start | bytes 466952 | tf_op jit(solution)/shard_map/ppermute | solution.py:543
  30.2 9.6 %collective-permute-start.11 = (bf16[224,128]{1,0:T(8,128)(2,1)S(1)}, bf16[224,128]{1,0:T(8,128)(2,1)S(1)}, u32[]{:S(2)}, u32[]{:S(2)}) collective-permute-start(bf16[224,128]{1,0:T(8,128)(2,1)S(1)} %get-tuple-element.34), channel_id=1, source_target_pairs={{0,48},{16,64},{32,80},{48,96},{64,112},{80,128},{96,144},{112,160... | collective-permute-start | bytes 172040 | tf_op jit(solution)/shard_map/ppermute | solution.py:543
  31.6 8.2 %collective-permute-start.12 = (bf16[224,128]{1,0:T(8,128)(2,1)S(1)}, bf16[224,128]{1,0:T(8,128)(2,1)S(1)}, u32[]{:S(2)}, u32[]{:S(2)}) collective-permute-start(bf16[224,128]{1,0:T(8,128)(2,1)S(1)} %get-tuple-element.35), channel_id=1, source_target_pairs={{0,208},{16,224},{32,240},{48,0},{64,16},{80,32},{96,48},{112,64},... | collective-permute-start | bytes 172040 | tf_op jit(solution)/shard_map/ppermute | solution.py:543
  34.4 10.7 %collective-permute-start.5 = (f32[128,128]{1,0:T(8,128)S(1)}, f32[128,128]{1,0:T(8,128)S(1)}, u32[]{:S(2)}, u32[]{:S(2)}) collective-permute-start(f32[128,128]{1,0:T(8,128)S(1)} %get-tuple-element.27), channel_id=1, source_target_pairs={{0,16},{16,32},{32,48},{48,64},{64,80},{80,96},{96,112},{112,128},... | collective-permute-start | bytes 196616 | tf_op jit(solution)/shard_map/ppermute | solution.py:543
  34.4 10.7 %collective-permute-start.6 = (f32[96,128]{1,0:T(8,128)S(1)}, f32[96,128]{1,0:T(8,128)S(1)}, u32[]{:S(2)}, u32[]{:S(2)}) collective-permute-start(f32[96,128]{1,0:T(8,128)S(1)} %get-tuple-element.28), channel_id=1, source_target_pairs={{0,240},{16,0},{32,16},{48,32},{64,48},{80,64},{96,80},{112,96},{1... | collective-permute-start | bytes 147464 | tf_op jit(solution)/shard_map/ppermute | solution.py:543
  40.0 32.1 %collective-permute-start.13 = (f32[672,128]{1,0:T(8,128)S(1)}, f32[672,128]{1,0:T(8,128)S(1)}, u32[]{:S(2)}, u32[]{:S(2)}) collective-permute-start(f32[672,128]{1,0:T(8,128)S(1)} %shard_map.138.near), channel_id=1, source_target_pairs={{0,1},{1,0},{2,3},{3,2},{4,5},{5,4},{6,7},{7,6},{8,9},{9,8},{10,11... | collective-permute-start | bytes 1032200 | tf_op jit(solution)/shard_map/ppermute | solution.py:543
  43.8 1.3 %collective-permute-start.7 = (f32[48,128]{1,0:T(8,128)S(1)}, f32[48,128]{1,0:T(8,128)S(1)}, u32[]{:S(2)}, u32[]{:S(2)}) collective-permute-start(f32[48,128]{1,0:T(8,128)S(1)} %get-tuple-element.29), channel_id=1, source_target_pairs={{0,1},{1,0},{2,3},{3,2},{4,5},{5,4},{6,7},{7,6},{8,9},{9,8},{10,11... | collective-permute-start | bytes 73736 | tf_op jit(solution)/shard_map/ppermute | solution.py:543
  66.4 6.7 %collective-permute-start.8 = (f32[96,128]{1,0:T(8,128)S(1)}, f32[96,128]{1,0:T(8,128)S(1)}, u32[]{:S(2)}, u32[]{:S(2)}) collective-permute-start(f32[96,128]{1,0:T(8,128)S(1)} %shard_map.136.own), channel_id=1, source_target_pairs={{0,1},{1,0},{2,3},{3,2},{4,5},{5,4},{6,7},{7,6},{8,9},{9,8},{10,11... | collective-permute-start | bytes 147464 | tf_op jit(solution)/shard_map/ppermute | solution.py:543
  72.0 1.2 %collective-permute-start.14 = (f32[32,128]{1,0:T(8,128)S(1)}, f32[32,128]{1,0:T(8,128)S(1)}, u32[]{:S(2)}, u32[]{:S(2)}) collective-permute-start(f32[32,128]{1,0:T(8,128)S(1)} %get-tuple-element.36.tips), channel_id=1, source_target_pairs={{0,1},{1,0},{2,3},{3,2},{4,5},{5,4},{6,7},{7,6},{8,9},{9,8},{10,11... | collective-permute-start | bytes 49160 | tf_op jit(solution)/shard_map/ppermute | solution.py:543
